TPU v7x, 32 devices: a whole 2x2x4 slice. The times are simulated.
32 devices in a mesh: seq: 16 (over z, y, core), ctx: 2 (over x).
Axes of the slice: x: 2, y: 2, z: 4, core: 2. Of those that a mesh axis runs over, the one named last changes fastest.
Arguments:
- tokens: bfloat16 [16, 256, 896], P('seq', 'ctx'), may hold values from -6 to 6
- positions: int32 [16, 256], P('seq'), may hold values from 0 to 255, as said below
- cotangent: bfloat16 [16, 256, 896], P('seq', 'ctx'), may hold values from -6 to 6
- qkv_weight: bfloat16 [896, 1152], P('seq'), may hold values from -0.1875 to 0.1875
- qkv_bias: bfloat16 [1152], P('seq'), may hold values from -16 to 16
- out_weight: bfloat16 [896, 896], P('seq'), may hold values from -0.75 to 0.75
- gate_up_weight: bfloat16 [896, 9728], P('seq'), may hold values from -0.1875 to 0.1875
- down_weight: bfloat16 [4864, 896], P('seq'), may hold values from -0.078125 to 0.078125
- attn_gain: bfloat16 [896], P('seq'), may hold values from 0.099609375 to 1.8984375
- ffn_gain: bfloat16 [896], P('seq'), may hold values from 0.099609375 to 1.8984375
Outputs:
- output: bfloat16 [16, 256, 896], P('seq', 'ctx')
- input_grad: float32 [16, 256, 896], P('seq', 'ctx')
- qkv_weight_grad: float32 [896, 1152], P('seq')
- qkv_bias_grad: float32 [1152], P('seq')
- out_weight_grad: float32 [896, 896], P('seq')
- gate_up_weight_grad: float32 [896, 9728], P('seq')
- down_weight_grad: float32 [4864, 896], P('seq')
- attn_gain_grad: float32 [896], P('seq')
- ffn_gain_grad: float32 [896], P('seq')
Inputs may be any that keep to these rules, and one draw needn't show every extreme that they name: Each sequence holds every position of 0 to 255 once. The 128 stored tokens of one index of ctx are two blocks of 64 consecutive positions in rising order, block b and block 3 - b, with b drawn for each sequence.
All inputs are finite; a program needn't handle non-finite values.
Results may differ from a plain program's by a relative error of at most 0.018.
The roundings to bfloat16 on the way count: a program that leaves them out, or rounds other values in their place, can miss the bound.
Values may be sent and summed in bfloat16 or wider, within the bound.
A program may use at most 192 MiB of HBM per device.

v0:
```python
import jax
import jax.numpy as jnp
from jax import lax
from jax.sharding import PartitionSpec as P

HEADS = 14
KV_HEADS = 2
HEAD_DIM = 64
FF = 4864


EPS = 1e-06
ROPE_BASE = 1000000.0


def to_bf16(values):
    return lax.optimization_barrier(values.astype(jnp.bfloat16))


def rope_tables(position_row):
    half_dim = HEAD_DIM // 2
    exponent = jnp.arange(half_dim, dtype=jnp.float32) * (2.0 / HEAD_DIM)
    inverse = ROPE_BASE ** (-exponent)
    angles = position_row.astype(jnp.float32)[:, None] * inverse[None, :]
    cosine_table = jnp.cos(angles)
    sine_table = jnp.sin(angles)
    return (
        jnp.concatenate([cosine_table, cosine_table], -1),
        jnp.concatenate([sine_table, sine_table], -1),
    )


def rotate_half(values):
    half_dim = values.shape[-1] // 2
    return jnp.concatenate([-values[..., half_dim:], values[..., :half_dim]], -1)


def rotate_back(values):
    half_dim = values.shape[-1] // 2
    return jnp.concatenate([values[..., half_dim:], -values[..., :half_dim]], -1)


def rms_forward(values):
    scaling = lax.rsqrt(jnp.mean(values * values, axis=-1, keepdims=True) + EPS)
    return (values * scaling, scaling)


def rms_backward(grad_normed, normed, scaling, gain_float):
    gain_grad = jnp.sum(grad_normed * normed, axis=0)
    grad_scaled = grad_normed * gain_float
    inner = jnp.mean(grad_scaled * normed, axis=-1, keepdims=True)
    return (scaling * (grad_scaled - normed * inner), gain_grad)


def weight_rows(left_side, right_side):
    return lax.psum_scatter(
        lax.dot_general(
            left_side, right_side, (((0,), (0,)), ((), ())), preferred_element_type=jnp.float32
        ),
        "seq",
        scatter_dimension=0,
        tiled=True,
    )


def shards(
    tokens,
    positions,
    cotangent,
    qkv_weight,
    qkv_bias,
    out_weight,
    gate_up_weight,
    down_weight,
    attn_gain,
    ffn_gain,
):
    f32 = jnp.float32
    gathered = (
        lax.all_gather(qkv_weight, "seq", axis=0, tiled=True),
        lax.all_gather(qkv_bias, "seq", axis=0, tiled=True),
        lax.all_gather(out_weight, "seq", axis=0, tiled=True),
        lax.all_gather(gate_up_weight, "seq", axis=0, tiled=True),
        lax.all_gather(down_weight, "seq", axis=0, tiled=True),
        lax.all_gather(attn_gain, "seq", axis=0, tiled=True),
        lax.all_gather(ffn_gain, "seq", axis=0, tiled=True),
    )
    full_qkv, full_bias, full_out, full_gate_up, full_down, gain_one, gain_two = gathered
    inputs_f = tokens[0].astype(f32)
    cot_row = cotangent[0]
    row_count = inputs_f.shape[0]
    group_size = HEADS // KV_HEADS
    query_width = HEADS * HEAD_DIM
    key_width = KV_HEADS * HEAD_DIM
    score_scale = HEAD_DIM ** (-0.5)
    all_positions = positions[0]
    position_row = lax.dynamic_slice_in_dim(
        all_positions, lax.axis_index("ctx") * row_count, row_count, 0
    )
    normed_one, scale_one = rms_forward(inputs_f)
    first_in = to_bf16(normed_one * gain_one.astype(f32))
    projected = jnp.dot(first_in, full_qkv, preferred_element_type=f32) + full_bias.astype(f32)
    cosine_table, sine_table = rope_tables(position_row)
    cos_query = cosine_table[:, None, None, :]
    sin_query = sine_table[:, None, None, :]
    cos_key = cosine_table[:, None, :]
    sin_key = sine_table[:, None, :]
    query = projected[:, :query_width].reshape(row_count, KV_HEADS, group_size, HEAD_DIM)
    keys = projected[:, query_width : query_width + key_width].reshape(
        row_count, KV_HEADS, HEAD_DIM
    )
    values = projected[:, query_width + key_width :]
    query_rot = to_bf16(query * cos_query + rotate_half(query) * sin_query)
    key_rot = to_bf16(keys * cos_key + rotate_half(keys) * sin_key).reshape(row_count, key_width)
    value_b = to_bf16(values)
    all_keys, all_values = (
        lax.all_gather(key_rot, "ctx", axis=0, tiled=True),
        lax.all_gather(value_b, "ctx", axis=0, tiled=True),
    )
    all_keys = all_keys.reshape(-1, KV_HEADS, HEAD_DIM)
    all_values = all_values.reshape(-1, KV_HEADS, HEAD_DIM)
    scores = (
        jnp.einsum("tkgd,skd->kgts", query_rot, all_keys, preferred_element_type=f32) * score_scale
    )
    allowed = all_positions[None, :] <= position_row[:, None]
    scores = jnp.where(allowed, scores, -1e30)
    row_top = jnp.max(scores, axis=-1, keepdims=True)
    log_total = row_top + jnp.log(jnp.sum(jnp.exp(scores - row_top), axis=-1, keepdims=True))
    probs = jnp.exp(scores - log_total)
    probs_b = to_bf16(probs)
    attended = to_bf16(
        jnp.einsum("kgts,skd->tkgd", probs_b, all_values, preferred_element_type=f32)
    )
    attended_flat = attended.reshape(row_count, query_width)
    residual = inputs_f + jnp.dot(attended_flat, full_out, preferred_element_type=f32)
    normed_two, scale_two = rms_forward(residual)
    second_in = to_bf16(normed_two * gain_two.astype(f32))
    gate_up = jnp.dot(second_in, full_gate_up, preferred_element_type=f32)
    gate = gate_up[:, :FF]
    upward = gate_up[:, FF:]
    activated = to_bf16(jax.nn.silu(gate) * upward)
    output_row = (residual + jnp.dot(activated, full_down, preferred_element_type=f32)).astype(
        jnp.bfloat16
    )
    back_qkv, back_bias, back_out, back_gate_up, back_down, back_gain_one, back_gain_two = gathered
    down_grad = weight_rows(activated, cot_row)
    grad_act = jnp.dot(cot_row, back_down.T, preferred_element_type=f32)
    sigmoid_gate = jax.nn.sigmoid(gate)
    grad_gate = grad_act * upward * sigmoid_gate * (1.0 + gate * (1.0 - sigmoid_gate))
    grad_upward = grad_act * jax.nn.silu(gate)
    grad_gate_up = to_bf16(jnp.concatenate([grad_gate, grad_upward], -1))
    gate_up_grad = weight_rows(second_in, grad_gate_up)
    grad_second = jnp.dot(grad_gate_up, back_gate_up.T, preferred_element_type=f32)
    grad_through, gain_two_grad = rms_backward(
        grad_second, normed_two, scale_two, back_gain_two.astype(f32)
    )
    grad_residual = cot_row.astype(f32) + grad_through
    grad_res_b = to_bf16(grad_residual)
    out_grad = weight_rows(attended_flat, grad_res_b)
    grad_attended = to_bf16(jnp.dot(grad_res_b, back_out.T, preferred_element_type=f32))
    grad_attended = grad_attended.reshape(row_count, KV_HEADS, group_size, HEAD_DIM)
    grad_probs = jnp.einsum("tkgd,skd->kgts", grad_attended, all_values, preferred_element_type=f32)
    delta = jnp.sum(grad_attended.astype(f32) * attended.astype(f32), axis=-1)
    delta = jnp.transpose(delta, (1, 2, 0))[..., None]
    grad_scores = to_bf16(probs * (grad_probs - delta) * score_scale)
    grad_query_rot = jnp.einsum("kgts,skd->tkgd", grad_scores, all_keys, preferred_element_type=f32)
    key_part = jnp.einsum("kgts,tkgd->skd", grad_scores, query_rot, preferred_element_type=f32)
    value_part = jnp.einsum("kgts,tkgd->skd", probs_b, grad_attended, preferred_element_type=f32)
    key_local = lax.psum_scatter(
        jnp.concatenate(
            [
                key_part.reshape(row_count * lax.axis_size("ctx"), key_width),
                value_part.reshape(row_count * lax.axis_size("ctx"), key_width),
            ],
            -1,
        ),
        "ctx",
        scatter_dimension=0,
        tiled=True,
    )
    grad_key_rot = key_local[:, :key_width].reshape(row_count, KV_HEADS, HEAD_DIM)
    grad_value = key_local[:, key_width:]
    grad_query = grad_query_rot * cos_query + rotate_back(grad_query_rot * sin_query)
    grad_key = grad_key_rot * cos_key + rotate_back(grad_key_rot * sin_key)
    grad_projected = jnp.concatenate(
        [
            grad_query.reshape(row_count, query_width),
            grad_key.reshape(row_count, key_width),
            grad_value,
        ],
        -1,
    )
    bias_grad = jnp.sum(grad_projected, axis=0)
    grad_proj_b = to_bf16(grad_projected)
    qkv_grad = weight_rows(first_in, grad_proj_b)
    grad_first = jnp.dot(grad_proj_b, back_qkv.T, preferred_element_type=f32)
    grad_input_part, gain_one_grad = rms_backward(
        grad_first, normed_one, scale_one, back_gain_one.astype(f32)
    )
    input_row_grad = grad_residual + grad_input_part
    bias_share, gain_one_share, gain_two_share = (
        lax.psum_scatter(bias_grad, "seq", scatter_dimension=0, tiled=True),
        lax.psum_scatter(gain_one_grad, "seq", scatter_dimension=0, tiled=True),
        lax.psum_scatter(gain_two_grad, "seq", scatter_dimension=0, tiled=True),
    )
    summed = lax.psum(
        (qkv_grad, bias_share, out_grad, gate_up_grad, down_grad, gain_one_share, gain_two_share),
        "ctx",
    )
    (
        result_qkv,
        result_bias,
        result_out,
        result_gate_up,
        result_down,
        result_gain_one,
        result_gain_two,
    ) = summed
    return (
        output_row[None],
        input_row_grad[None],
        result_qkv,
        result_bias,
        result_out,
        result_gate_up,
        result_down,
        result_gain_one,
        result_gain_two,
    )


def solution(mesh):
    in_specs = (
        P("seq", "ctx", None),
        P("seq", None),
        P("seq", "ctx", None),
        P("seq", None),
        P("seq"),
        P("seq", None),
        P("seq", None),
        P("seq", None),
        P("seq"),
        P("seq"),
    )
    out_specs = (
        P("seq", "ctx", None),
        P("seq", "ctx", None),
        P("seq", None),
        P("seq"),
        P("seq", None),
        P("seq", None),
        P("seq", None),
        P("seq"),
        P("seq"),
    )
    return jax.shard_map(shards, mesh=mesh, in_specs=in_specs, out_specs=out_specs, check_vma=False)
```

profile of v0, /device:TPU:0, one launch (start us, length us, event | category | flops | bytes accessed | tf_op | source)
XLA Modules:
  0.0 1105.2 jit_solution(8537718753763260403)
XLA Ops:
  15.2 36.0 %all-reduce.11 = (bf16[896]{0:T(1024)(128)(2,1)S(1)}, bf16[1152]{0:T(1024)(128)(2,1)S(1)}, bf16[896]{0:T(1024)(128)(2,1)S(1)}) all-reduce(bf16[896]{0:T(1024)(128)(2,1)S(1)} %dynamic-update-slice, bf16[1152]{0:T(1024)(128)(2,1)S(1)} %dynamic-update-slice.1, bf16[896]{0:T(1024)(128)(2,1)S(1)} %dynamic-update-slice.2), channel_id=1, replica_groups=mesh['seq'=16,'ctx'=2] {'seq'}, use_global_device_ids=true, to_apply=%add | all-reduce | flops 2944 | bytes 11776
  52.8 1.8 all-gather.5.cloned.1.call-done
  54.5 2.1 convolution_add_fusion
  56.7 4.6 all_gather.30
  62.5 4.8 all_gather.31
  69.5 25.7 %all-gather.7.cloned.1.call-done = bf16[896,896]{1,0:T(8,128)(2,1)} async-done(((bf16[56,896]{1,0:T(8,128)(2,1)}), bf16[896,896]{1,0:T(8,128)(2,1)}) %all-gather.7.cloned.1.call-update) | async-done | bytes 1605648 | tf_op jit(solution)/shard_map/all_gather | solution.py:82
  95.2 2.1 multiply_reduce_fusion.3
  98.1 89.5 %all-gather.9.cloned.1.call-done = bf16[896,9728]{1,0:T(8,128)(2,1)} async-done(((bf16[56,9728]{1,0:T(8,128)(2,1)}), bf16[896,9728]{1,0:T(8,128)(2,1)}) %all-gather.9.cloned.1.call-update) | async-done | bytes 17432592 | tf_op jit(solution)/shard_map/all_gather | solution.py:83
  187.7 11.1 %fusion.37 = f32[128,9728]{1,0:T(8,128)} fusion(bf16[128,896]{1,0:T(8,128)(2,1)} %multiply_convert_fusion.3, bf16[896,9728]{1,0:T(8,128)(2,1)} %all-gather.9.cloned.1.call-done), kind=kOutput, calls=%fused_computation.86 | convolution fusion | flops 2231369728 | bytes 22642688 | tf_op jit(solution)/shard_map/dot_general | solution.py:138
  198.8 67.3 %all-gather.11.cloned.1.call-done = bf16[4864,896]{1,0:T(8,128)(2,1)} async-done(((bf16[304,896]{1,0:T(8,128)(2,1)}), bf16[4864,896]{1,0:T(8,128)(2,1)}) %all-gather.11.cloned.1.call-update) | async-done | bytes 8716304 | tf_op jit(solution)/shard_map/all_gather | solution.py:84
  266.0 8.5 multiply_convert_fusion.1
  274.6 1.6 pad_maximum_fusion
  276.2 12.9 %multiply_reduce_fusion = (f32[896]{0:T(1024)S(1)}, f32[128]{0:T(128)S(1)}, f32[128,896]{1,0:T(8,128)}) fusion(f32[128,896]{1,0:T(8,128)S(1)} %get-tuple-element.49, f32[128]{0:T(128)S(1)} %add_rsqrt_fusion, f32[896]{0:T(1024)S(1)} %convert_element_type.85, bf16[128,9728]{1,0:T(8,128)(2,1)} %pad_maximum_fusion, ...), kind=kOutput, calls=%fused_computation.42 | convolution fusion | flops 2232056832 | bytes 20848640 | tf_op jit(solution)/shard_map/dot_general | solution.py:153
  291.1 2.7 convolution_convert_fusion
  293.8 1.8 copy.47
  301.9 2.3 fusion.41
  305.7 6.5 reduce-scatter.10.cloned.1.call-done
  314.5 2.8 fusion.40
  318.6 7.6 fusion.24
  326.3 1.7 copy-done
  327.9 14.0 %fusion.42 = f32[896,9728]{1,0:T(8,128)} fusion(bf16[128,896]{1,0:T(8,128)(2,1)S(1)} %copy-done.11, bf16[128,9728]{1,0:T(8,128)(2,1)S(1)} %copy-done), kind=kOutput, calls=%fused_computation.91 | convolution fusion | flops 2231369728 | bytes 37584896 | tf_op jit(solution)/shard_map/dot_general | solution.py:57
  342.0 42.1 %reduce-scatter.18.cloned.1.call-done = f32[56,896]{1,0:T(8,128)} async-done(((f32[896,896]{1,0:T(8,128)}), f32[56,896]{1,0:T(8,128)}) %reduce-scatter.18.cloned.1.call-update) | async-done | bytes 200720
  384.1 73.5 %reduce-scatter.16.cloned.1.call-done = f32[56,1152]{1,0:T(8,128)} async-done(((f32[896,1152]{1,0:T(8,128)}), f32[56,1152]{1,0:T(8,128)}) %reduce-scatter.16.cloned.1.call-update) | async-done | bytes 258064
  457.6 186.5 %reduce-scatter.14.cloned.1.call-done = f32[304,896]{1,0:T(8,128)} async-done(((f32[4864,896]{1,0:T(8,128)}), f32[304,896]{1,0:T(8,128)}) %reduce-scatter.14.cloned.1.call-update) | async-done | bytes 1089552 | tf_op jit(solution)/shard_map/reduce_scatter | solution.py:56
  644.1 346.6 %reduce-scatter.12.cloned.1.call-done = f32[56,9728]{1,0:T(8,128)} async-done(((f32[896,9728]{1,0:T(8,128)}), f32[56,9728]{1,0:T(8,128)}) %reduce-scatter.12.cloned.1.call-update) | async-done | bytes 2179088 | tf_op jit(solution)/shard_map/reduce_scatter | solution.py:56
  992.1 5.8 fusion.7
  999.1 59.5 %all-reduce.8 = (f32[1152]{0:T(1024)S(1)}, f32[896]{0:T(1024)S(1)}, f32[896]{0:T(1024)S(1)}) all-reduce(f32[1152]{0:T(1024)S(1)} %fusion.22, f32[896]{0:T(1024)S(1)} %get-tuple-element.11, f32[896]{0:T(1024)S(1)} %get-tuple-element.9), channel_id=4, replica_groups=mesh['seq'=16,'ctx'=2] {'seq'}, use_global_device_ids=true, to_apply=%region_11.12.clone | all-reduce | flops 2944 | bytes 23552
  1058.8 5.6 all-reduce.9
  1065.5 25.4 %all-reduce.14.cloned.1.call-done = (f32[56,1152]{1,0:T(8,128)}, f32[56,896]{1,0:T(8,128)}, f32[56,9728]{1,0:T(8,128)}, f32[304,896]{1,0:T(8,128)}) async-done(((f32[56,1152]{1,0:T(8,128)}, f32[56,896]{1,0:T(8,128)}, f32[56,9728]{1,0:T(8,128)}, f32[304,896]{1,0:T(8,128)}), (f32[56,1152]{1,0:T(8,128)}, f32[56,896]{1,0:T(8,128)}, f32[56,9728]{1,0:T(8,128)}, ...) | async-done | bytes 3727376 | tf_op jit(solution)/shard_map/psum | solution.py:206
  1090.9 1.7 copy.66
  1092.6 1.6 copy.67
  1094.2 3.2 copy.68
  (136 shorter events, 29.0 us)
Async XLA Ops:
  7.2 45.1 %copy-start.6 = (bf16[1,128,896]{2,1,0:T(8,128)(2,1)S(1)}, bf16[1,128,896]{2,1,0:T(8,128)(2,1)}, u32[]{:S(2)}) copy-start(bf16[1,128,896]{2,1,0:T(8,128)(2,1)} %param.10) | copy-start | bytes 688132
  7.2 45.3 %copy-start.28 = (s32[1,256]{1,0:T(1,128)S(1)}, s32[1,256]{1,0:T(1,128)}, u32[]{:S(2)}) copy-start(s32[1,256]{1,0:T(1,128)} %param.11) | copy-start | bytes 3076
  7.2 47.3 %all-gather.5.cloned.1.call-start = ((), (), s32[]{:S(2)}) async-start(), calls=%async_computation.5 | async-start | bytes 2193408 | tf_op jit(solution)/shard_map/all_gather | solution.py:80
  7.9 87.3 %all-gather.7.cloned.1.call-start = ((), (), s32[]{:S(2)}) async-start(), calls=%async_computation.6 | async-start | bytes 1705984 | tf_op jit(solution)/shard_map/all_gather | solution.py:82
  8.7 179.0 %all-gather.9.cloned.1.call-start = ((), (), s32[]{:S(2)}) async-start(), calls=%async_computation.7 | async-start | bytes 18522112 | tf_op jit(solution)/shard_map/all_gather | solution.py:83
  9.4 256.6 %all-gather.11.cloned.1.call-start = ((), (), s32[]{:S(2)}) async-start(), calls=%async_computation.8 | async-start | bytes 9261056 | tf_op jit(solution)/shard_map/all_gather | solution.py:84
  10.0 302.3 %reduce-scatter.10.cloned.1.call-start = ((), (), s32[]{:S(2)}) async-start(), calls=%async_computation.9 | async-start | bytes 393216 | tf_op jit(solution)/shard_map/reduce_scatter | solution.py:169
  52.4 9.6 copy-start.20
  62.5 5.5 copy-start.18
  295.6 5.1 copy-start.19
  298.1 3.8 copy-start.10
  298.1 3.8 copy-start.17
  301.8 82.3 %reduce-scatter.18.cloned.1.call-start = ((), (), s32[]{:S(2)}) async-start(), calls=%async_computation.13 | async-start | bytes 3411968
  304.2 1.2 copy-start.27
  304.2 153.4 %reduce-scatter.16.cloned.1.call-start = ((), (), s32[]{:S(2)}) async-start(), calls=%async_computation.12 | async-start | bytes 4386816
  305.6 8.9 copy-start.21
  305.7 7.5 copy-start.7
  317.3 1.3 copy-start.1
  317.3 1.3 copy-start.14
  317.3 326.8 %reduce-scatter.14.cloned.1.call-start = ((), (), s32[]{:S(2)}) async-start(), calls=%async_computation.11 | async-start | bytes 18522112 | tf_op jit(solution)/shard_map/reduce_scatter | solution.py:56
  326.2 1.7 copy-start
  326.2 1.7 copy-start.11
  326.2 664.6 %reduce-scatter.12.cloned.1.call-start = ((), (), s32[]{:S(2)}) async-start(), calls=%async_computation.10 | async-start | bytes 37044224 | tf_op jit(solution)/shard_map/reduce_scatter | solution.py:56
  341.9 650.2 %copy-start.2 = (bf16[128,4864]{1,0:T(8,128)(2,1)S(1)}, bf16[128,4864]{1,0:T(8,128)(2,1)}, u32[]{:S(2)}) copy-start(bf16[128,4864]{1,0:T(8,128)(2,1)} %get-tuple-element.30) | copy-start | bytes 3735556
  341.9 749.0 %all-reduce.14.cloned.1.call-start = ((), (), s32[]{:S(2)}) async-start(), calls=%async_computation.14 | async-start | bytes 7454720 | tf_op jit(solution)/shard_map/psum | solution.py:206
  992.1 5.8 copy-start.8
  992.1 5.8 copy-start.25
  992.1 6.1 copy-start.5
  992.1 6.1 copy-start.13
  997.9 66.5 %copy-start.9 = (f32[128,896]{1,0:T(8,128)S(1)}, f32[128,896]{1,0:T(8,128)}, u32[]{:S(2)}) copy-start(f32[128,896]{1,0:T(8,128)} %get-tuple-element.50) | copy-start | bytes 1376260
  997.9 66.5 %copy-start.15 = (bf16[1,128,896]{2,1,0:T(8,128)(2,1)S(1)}, bf16[1,128,896]{2,1,0:T(8,128)(2,1)}, u32[]{:S(2)}) copy-start(bf16[1,128,896]{2,1,0:T(8,128)(2,1)} %param.12) | copy-start | bytes 688132
  1094.2 3.2 copy-start.22
  (7 other events, 5.8 us)
Sparse Core Ops, SparseCore 0:
  10.2 44.2 all-gather.4
  56.7 38.5 all-gather.6
  96.8 90.7 all-gather.8
  189.7 76.3 all-gather.10
  301.9 10.2 reduce-scatter.9
  316.0 68.0 reduce-scatter.17
  388.0 69.5 reduce-scatter.15
  461.8 182.3 reduce-scatter.13
  648.4 342.2 reduce-scatter.11
  993.1 97.7 all-reduce.13
where the time goes:
time: 1110 us
  waiting for transfers between devices  868 us (78%)
  blocking collectives  110 us (10%)
  matrix products  77.8 us (7%)
  local copies, waits for them, and re-layouts  21.4 us (2%)
  between operations  17.3 us (2%)
    reduce_scatter x2, waiting for transfers between devices, weight_rows(): lax.psum_scatter(lax.dot_general(left_side, right_side, (((0,), (0,)), ((...  533 us
    unnamed x12, waiting for transfers between devices  118 us
    unnamed x2, blocking collectives  95.5 us
    all_gather x1, waiting for transfers between devices, shards(): lax.all_gather(gate_up_weight, 'seq', axis=0, tiled=True)  89.5 us
    all_gather x1, waiting for transfers between devices, shards(): lax.all_gather(down_weight, 'seq', axis=0, tiled=True)  67.3 us
    dot_general x4, matrix products, weight_rows(): lax.dot_general(left_side, right_side, (((0,), (0,)), ((), ())), preferre...  26.6 us
    all_gather x1, waiting for transfers between devices, shards(): lax.all_gather(out_weight, 'seq', axis=0, tiled=True)  25.7 us
    psum x1, waiting for transfers between devices, shards(): lax.psum((qkv_grad, bias_share, out_grad, gate_up_grad, down_grad, gain_o...  25.4 us
  transfers between devices with their start and end apart: 10, of which 10 were waited for; matrix products, arithmetic and copies ran while one was open for 5% of the time, Pallas kernels for 0%

commit v1 on v0

--- a/solution.py
+++ b/solution.py
@@ -6,7 +6,6 @@
 HEADS = 14
 KV_HEADS = 2
 HEAD_DIM = 64
-FF = 4864
 
 
 EPS = 1e-06
@@ -61,6 +60,40 @@
         scatter_dimension=0,
         tiled=True,
     )
+
+
+def columns_from_rows(rows, parts):
+    depth = rows.shape[0]
+    hidden = rows.shape[1] // (2 * parts)
+    split = jnp.transpose(rows.reshape(depth, 2, parts, hidden), (2, 0, 1, 3))
+    split = split.reshape(parts, depth, 2 * hidden)
+    moved = lax.all_to_all(split, "seq", split_axis=0, concat_axis=0, tiled=True)
+    return moved.reshape(parts * depth, 2 * hidden)
+
+
+def rows_from_columns(columns, parts):
+    depth = columns.shape[0] // parts
+    hidden = columns.shape[1] // 2
+    split = columns.reshape(parts, depth, 2 * hidden)
+    moved = lax.all_to_all(split, "seq", split_axis=0, concat_axis=0, tiled=True)
+    moved = jnp.transpose(moved.reshape(parts, depth, 2, hidden), (1, 2, 0, 3))
+    return moved.reshape(depth, 2 * parts * hidden)
+
+
+def contract_rows(left_side, right_side):
+    return lax.dot_general(
+        left_side, right_side, (((0,), (0,)), ((), ())), preferred_element_type=jnp.float32
+    )
+
+
+def contract_columns(left_side, right_side):
+    return lax.dot_general(
+        left_side, right_side, (((1,), (1,)), ((), ())), preferred_element_type=jnp.float32
+    )
+
+
+def scatter_tokens(partial):
+    return lax.psum_scatter(partial, "seq", scatter_dimension=0, tiled=True)
 
 
 def shards(
@@ -80,12 +113,14 @@
         lax.all_gather(qkv_weight, "seq", axis=0, tiled=True),
         lax.all_gather(qkv_bias, "seq", axis=0, tiled=True),
         lax.all_gather(out_weight, "seq", axis=0, tiled=True),
-        lax.all_gather(gate_up_weight, "seq", axis=0, tiled=True),
-        lax.all_gather(down_weight, "seq", axis=0, tiled=True),
         lax.all_gather(attn_gain, "seq", axis=0, tiled=True),
         lax.all_gather(ffn_gain, "seq", axis=0, tiled=True),
     )
-    full_qkv, full_bias, full_out, full_gate_up, full_down, gain_one, gain_two = gathered
+    full_qkv, full_bias, full_out, gain_one, gain_two = gathered
+    parts = lax.axis_size("seq")
+    hidden = down_weight.shape[0]
+    own_gate_up = columns_from_rows(gate_up_weight, parts)
+    all_cot = lax.all_gather(cotangent[0], "seq", axis=0, tiled=True)
     inputs_f = tokens[0].astype(f32)
     cot_row = cotangent[0]
     row_count = inputs_f.shape[0]
@@ -135,29 +170,29 @@
     residual = inputs_f + jnp.dot(attended_flat, full_out, preferred_element_type=f32)
     normed_two, scale_two = rms_forward(residual)
     second_in = to_bf16(normed_two * gain_two.astype(f32))
-    gate_up = jnp.dot(second_in, full_gate_up, preferred_element_type=f32)
-    gate = gate_up[:, :FF]
-    upward = gate_up[:, FF:]
-    activated = to_bf16(jax.nn.silu(gate) * upward)
-    output_row = (residual + jnp.dot(activated, full_down, preferred_element_type=f32)).astype(
-        jnp.bfloat16
-    )
-    back_qkv, back_bias, back_out, back_gate_up, back_down, back_gain_one, back_gain_two = gathered
-    down_grad = weight_rows(activated, cot_row)
-    grad_act = jnp.dot(cot_row, back_down.T, preferred_element_type=f32)
+    all_second = lax.all_gather(second_in, "seq", axis=0, tiled=True)
+    gate_up = jnp.dot(all_second, own_gate_up, preferred_element_type=f32)
+    gate = gate_up[:, :hidden]
+    upward = gate_up[:, hidden:]
     sigmoid_gate = jax.nn.sigmoid(gate)
+    activated = to_bf16(gate * sigmoid_gate * upward)
+    grad_act = contract_columns(all_cot, down_weight)
     grad_gate = grad_act * upward * sigmoid_gate * (1.0 + gate * (1.0 - sigmoid_gate))
-    grad_upward = grad_act * jax.nn.silu(gate)
+    grad_upward = grad_act * (gate * sigmoid_gate)
     grad_gate_up = to_bf16(jnp.concatenate([grad_gate, grad_upward], -1))
-    gate_up_grad = weight_rows(second_in, grad_gate_up)
-    grad_second = jnp.dot(grad_gate_up, back_gate_up.T, preferred_element_type=f32)
+    grad_second = scatter_tokens(contract_columns(grad_gate_up, own_gate_up))
+    output_row = (
+        residual + scatter_tokens(jnp.dot(activated, down_weight, preferred_element_type=f32))
+    ).astype(jnp.bfloat16)
+    down_grad = contract_rows(activated, all_cot)
+    gate_up_grad = rows_from_columns(contract_rows(all_second, grad_gate_up), parts)
     grad_through, gain_two_grad = rms_backward(
-        grad_second, normed_two, scale_two, back_gain_two.astype(f32)
+        grad_second, normed_two, scale_two, gain_two.astype(f32)
     )
     grad_residual = cot_row.astype(f32) + grad_through
     grad_res_b = to_bf16(grad_residual)
     out_grad = weight_rows(attended_flat, grad_res_b)
-    grad_attended = to_bf16(jnp.dot(grad_res_b, back_out.T, preferred_element_type=f32))
+    grad_attended = to_bf16(jnp.dot(grad_res_b, full_out.T, preferred_element_type=f32))
     grad_attended = grad_attended.reshape(row_count, KV_HEADS, group_size, HEAD_DIM)
     grad_probs = jnp.einsum("tkgd,skd->kgts", grad_attended, all_values, preferred_element_type=f32)
     delta = jnp.sum(grad_attended.astype(f32) * attended.astype(f32), axis=-1)
@@ -193,9 +228,9 @@
     bias_grad = jnp.sum(grad_projected, axis=0)
     grad_proj_b = to_bf16(grad_projected)
     qkv_grad = weight_rows(first_in, grad_proj_b)
-    grad_first = jnp.dot(grad_proj_b, back_qkv.T, preferred_element_type=f32)
+    grad_first = jnp.dot(grad_proj_b, full_qkv.T, preferred_element_type=f32)
     grad_input_part, gain_one_grad = rms_backward(
-        grad_first, normed_one, scale_one, back_gain_one.astype(f32)
+        grad_first, normed_one, scale_one, gain_one.astype(f32)
     )
     input_row_grad = grad_residual + grad_input_part
     bias_share, gain_one_share, gain_two_share = (

time: 1110 us -> 717 us (0.65)
  waiting for transfers between devices: 868 us -> 422 us
  blocking collectives: 110 us -> 158 us
  matrix products: 77.8 us -> 55.1 us
  local copies, waits for them, and re-layouts: 21.4 us -> 42.6 us
    reduce_scatter x2, waiting for transfers between devices: 533 us -> 114 us  [scatter_tokens(): return lax.psum_scatter(partial, 'seq', scatter_dimension=0, tiled=True)]
    all_gather x2, waiting for transfers between devices: 157 us -> 40.3 us  [the longest x1 40.3 us: shards(): all_cot = lax.all_gather(cotangent[0], 'seq', axis=0, tiled=True)]
    psum x1, waiting for transfers between devices: 25.4 us -> 98.9 us  [shards(): lax.psum((qkv_grad, bias_share, out_grad, gate_up_grad, down_grad, gain_o...]
    all_to_all x0 -> x1, waiting for transfers between devices: none -> 52.4 us  [rows_from_columns(): lax.all_to_all(split, 'seq', split_axis=0, concat_axis=0, tiled=True)]
    all_to_all x0 -> x1, blocking collectives: none -> 48.1 us  [columns_from_rows(): lax.all_to_all(split, 'seq', split_axis=0, concat_axis=0, tiled=True)]
    unnamed x12, waiting for transfers between devices: 118 us -> 81.2 us
    dot_general x4 -> x2, matrix products: 26.6 us -> 5.08 us  [weight_rows(): lax.dot_general(left_side, right_side, (((0,), (0,)), ((), ())), preferre...]
    reshape x0 -> x5, local copies, waits for them, and re-layouts: none -> 19.2 us  [the longest x2 7.89 us: columns_from_rows(): split = jnp.transpose(rows.reshape(depth, 2, parts, hidden), (2, 0, 1, 3))]
  transfers between devices with their start and end apart: 10 -> 11, of which waited for: 10 -> 10; matrix products, arithmetic and copies ran while one was open for 5% -> 10% of each run, Pallas kernels for 0% -> 0%
where the time goes in v1:
time: 717 us; the launch traced here: 716 us
  waiting for transfers between devices  422 us (59%)
  blocking collectives  158 us (22%)
  matrix products  55.1 us (8%)
  local copies, waits for them, and re-layouts  42.6 us (6%)
  between operations  17.5 us (2%)
  other arithmetic  14.6 us (2%)
    reduce_scatter x2, waiting for transfers between devices, scatter_tokens(): return lax.psum_scatter(partial, 'seq', scatter_dimension=0, tiled=True)  114 us
    psum x1, waiting for transfers between devices, shards(): lax.psum((qkv_grad, bias_share, out_grad, gate_up_grad, down_grad, gain_o...  98.9 us
    unnamed x2, blocking collectives  95.3 us
    unnamed x12, waiting for transfers between devices  81.2 us
    all_to_all x1, waiting for transfers between devices, rows_from_columns(): lax.all_to_all(split, 'seq', split_axis=0, concat_axis=0, tiled=True)  52.4 us
    all_to_all x1, blocking collectives, columns_from_rows(): lax.all_to_all(split, 'seq', split_axis=0, concat_axis=0, tiled=True)  48.1 us
    all_gather x1, waiting for transfers between devices, shards(): all_cot = lax.all_gather(cotangent[0], 'seq', axis=0, tiled=True)  40.3 us
    all_gather x1, waiting for transfers between devices, shards(): lax.all_gather(out_weight, 'seq', axis=0, tiled=True)  26.4 us
  transfers between devices with their start and end apart: 11, of which 10 were waited for; matrix products, arithmetic and copies ran while one was open for 10% of the time, Pallas kernels for 0%

profile of v1, /device:TPU:0, one launch (start us, length us, event | category | flops | bytes accessed | tf_op | source)
XLA Modules:
  0.0 715.8 jit_solution(11710058822205931691)
XLA Ops:
  15.0 35.9 %all-reduce.11 = (bf16[896]{0:T(1024)(128)(2,1)S(1)}, bf16[1152]{0:T(1024)(128)(2,1)S(1)}, bf16[896]{0:T(1024)(128)(2,1)S(1)}) all-reduce(bf16[896]{0:T(1024)(128)(2,1)S(1)} %dynamic-update-slice, bf16[1152]{0:T(1024)(128)(2,1)S(1)} %dynamic-update-slice.1, bf16[896]{0:T(1024)(128)(2,1)S(1)} %dynamic-update-slice.2), channel_id=1, replica_groups=mesh['seq'=16,'ctx'=2] {'seq'}, use_global_device_ids=true, to_apply=%add | all-reduce | flops 2944 | bytes 11776
  56.7 4.6 all_gather.30
  61.9 4.6 all_gather.31
  68.7 26.4 %all-gather.8.cloned.1.call-done = bf16[896,896]{1,0:T(8,128)(2,1)} async-done(((bf16[56,896]{1,0:T(8,128)(2,1)}), bf16[896,896]{1,0:T(8,128)(2,1)}) %all-gather.8.cloned.1.call-update) | async-done | bytes 1605648 | tf_op jit(solution)/shard_map/all_gather | solution.py:115
  98.6 4.3 reshape.135
  103.0 3.6 copy.68
  106.5 4.1 reshape.136
  110.6 48.1 %all_to_all.10 = bf16[16,56,608]{2,1,0:T(8,128)(2,1)} all-to-all(bf16[16,56,608]{2,1,0:T(8,128)(2,1)} %reshape.136), channel_id=1, replica_groups=mesh['seq'=16,'ctx'=2] {'seq'}, dimensions={0} | all-to-all | bytes 2179072 | tf_op jit(solution)/shard_map/all_to_all | solution.py:70
  158.7 7.4 %fusion.36 = f32[2048,608]{0,1:T(8,128)} fusion(bf16[2048,896]{1,0:T(8,128)(2,1)} %all-gather.10.cloned.1.call-done, bf16[896,608]{1,0:T(8,128)(2,1)} %bitcast.134), kind=kOutput, calls=%fused_computation.86 | convolution fusion | flops 2231369728 | bytes 9740288 | tf_op jit(solution)/shard_map/dot_general | solution.py:174
  166.1 40.3 %all-gather.12.cloned.1.call-done = bf16[1,2048,896]{2,1,0:T(8,128)(2,1)} async-done(((bf16[1,128,896]{2,1,0:T(8,128)(2,1)}), bf16[1,2048,896]{2,1,0:T(8,128)(2,1)}) %all-gather.12.cloned.1.call-update) | async-done | bytes 3670032 | tf_op jit(solution)/shard_map/all_gather | solution.py:123
  206.4 6.8 multiply_convert_fusion.1
  214.8 5.5 fusion.38
  220.4 90.4 %reduce-scatter.12.cloned.1.call-done = f32[128,896]{1,0:T(8,128)} async-done(((f32[2048,896]{1,0:T(8,128)}), f32[128,896]{1,0:T(8,128)}) %reduce-scatter.12.cloned.1.call-update) | async-done | bytes 458768 | tf_op jit(solution)/shard_map/reduce_scatter | solution.py:96
  325.8 7.7 %reduce-scatter.14.cloned.1.call-done = f32[128,256]{0,1:T(8,128)} async-done(((f32[256,256]{0,1:T(8,128)}), f32[128,256]{0,1:T(8,128)}) %reduce-scatter.14.cloned.1.call-update) | async-done | bytes 131088 | tf_op jit(solution)/shard_map/reduce_scatter | solution.py:204
  334.6 2.8 fusion.41
  338.7 5.2 fusion.37
  343.9 7.6 %fusion.43 = f32[896,608]{1,0:T(8,128)} fusion(bf16[2048,896]{1,0:T(8,128)(2,1)} %all-gather.10.cloned.1.call-done, bf16[2048,608]{0,1:T(8,128)(2,1)} %copy-done.9), kind=kOutput, calls=%fused_computation.93 | convolution fusion | flops 2231369728 | bytes 8339456 | tf_op jit(solution)/shard_map/dot_general | solution.py:84
  351.6 5.6 all-to-all-start.1
  357.2 4.9 fusion
  362.0 52.4 %all-to-all-done.1 = f32[16,56,608]{2,1,0:T(8,128)S(1)} async-done(((f32[16,56,608]{2,1,0:T(8,128)}), f32[16,56,608]{2,1,0:T(8,128)S(1)}, u32[]{:S(2)}, u32[]{:S(2)}) %all-to-all-start.1) | async-done | bytes 2179104 | tf_op jit(solution)/shard_map/all_to_all | solution.py:78
  414.4 3.1 reshape.144
  417.5 4.2 copy.57
  421.7 4.2 reshape.145
  425.8 5.9 reduce-scatter.18.cloned.1.call-done
  431.7 73.3 %reduce-scatter.16.cloned.1.call-done = f32[56,1152]{1,0:T(8,128)} async-done(((f32[896,1152]{1,0:T(8,128)}), f32[56,1152]{1,0:T(8,128)}) %reduce-scatter.16.cloned.1.call-update) | async-done | bytes 258064
  507.9 3.0 fusion.20
  510.9 59.4 %all-reduce.8 = (f32[1152]{0:T(1024)S(1)}, f32[896]{0:T(1024)S(1)}, f32[896]{0:T(1024)S(1)}) all-reduce(f32[1152]{0:T(1024)S(1)} %fusion.24, f32[896]{0:T(1024)S(1)} %get-tuple-element.11, f32[896]{0:T(1024)S(1)} %get-tuple-element.9), channel_id=7, replica_groups=mesh['seq'=16,'ctx'=2] {'seq'}, use_global_device_ids=true, to_apply=%region_13.14.clone | all-reduce | flops 2944 | bytes 23552
  570.6 5.4 all-reduce.9
  576.6 23.6 %reduce-scatter.10.cloned.1.call-done = f32[128,896]{1,0:T(8,128)} async-done(((f32[2048,896]{1,0:T(8,128)}), f32[128,896]{1,0:T(8,128)}) %reduce-scatter.10.cloned.1.call-update) | async-done | bytes 458768 | tf_op jit(solution)/shard_map/reduce_scatter | solution.py:96
  600.2 2.4 fusion.19
  602.6 98.9 %all-reduce.14.cloned.1.call-done = (f32[56,1152]{1,0:T(8,128)}, f32[56,896]{1,0:T(8,128)}, f32[56,9728]{1,0:T(8,128)}, f32[304,896]{1,0:T(8,128)}) async-done(((f32[56,1152]{1,0:T(8,128)}, f32[56,896]{1,0:T(8,128)}, f32[56,9728]{1,0:T(8,128)}, f32[304,896]{1,0:T(8,128)}), (f32[56,1152]{1,0:T(8,128)}, f32[56,896]{1,0:T(8,128)}, f32[56,9728]{1,0:T(8,128)}, ...) | async-done | bytes 3727376 | tf_op jit(solution)/shard_map/psum | solution.py:241
  704.8 3.2 copy.78
  (150 shorter events, 43.6 us)
Async XLA Ops:
  7.2 199.2 %copy-start = (bf16[304,896]{1,0:T(8,128)(2,1)S(1)}, bf16[304,896]{1,0:T(8,128)(2,1)}, u32[]{:S(2)}) copy-start(bf16[304,896]{1,0:T(8,128)(2,1)} %param.17) | copy-start | bytes 1634308
  7.2 47.3 %all-gather.6.cloned.1.call-start = ((), (), s32[]{:S(2)}) async-start(), calls=%async_computation.7 | async-start | bytes 2193408 | tf_op jit(solution)/shard_map/all_gather | solution.py:113
  7.9 87.2 %all-gather.8.cloned.1.call-start = ((), (), s32[]{:S(2)}) async-start(), calls=%async_computation.8 | async-start | bytes 1705984 | tf_op jit(solution)/shard_map/all_gather | solution.py:115
  8.7 150.0 %all-gather.10.cloned.1.call-start = ((), (), s32[]{:S(2)}) async-start(), calls=%async_computation.9 | async-start | bytes 3899392 | tf_op jit(solution)/shard_map/all_gather | solution.py:173
  12.5 40.3 %copy-start.29 = (f32[128]{0:T(128)}, f32[128]{0:T(128)S(1)}, u32[]{:S(2)}) copy-start(f32[128]{0:T(128)S(1)} %add_rsqrt_fusion.1) | copy-start | bytes 1540
  52.1 4.6 copy-start.16
  53.0 8.8 %copy-start.20 = (f32[128,64]{0,1:T(8,128)}, f32[128,64]{0,1:T(8,128)S(1)}, u32[]{:S(2)}) copy-start(f32[128,64]{0,1:T(8,128)S(1)} %get-tuple-element.56) | copy-start | bytes 98308
  53.0 8.8 %copy-start.22 = (f32[128,64]{0,1:T(8,128)}, f32[128,64]{0,1:T(8,128)S(1)}, u32[]{:S(2)}) copy-start(f32[128,64]{0,1:T(8,128)S(1)} %get-tuple-element.55) | copy-start | bytes 98308
  61.4 6.2 copy-start.25
  61.9 4.6 copy-start.14
  67.2 27.9 %copy-start.6 = (bf16[1,128,896]{2,1,0:T(8,128)(2,1)S(1)}, bf16[1,128,896]{2,1,0:T(8,128)(2,1)}, u32[]{:S(2)}) copy-start(bf16[1,128,896]{2,1,0:T(8,128)(2,1)} %param.10) | copy-start | bytes 688132
  98.0 108.4 %all-gather.12.cloned.1.call-start = ((), (), s32[]{:S(2)}) async-start(), calls=%async_computation.13 | async-start | bytes 3899392 | tf_op jit(solution)/shard_map/all_gather | solution.py:123
  98.6 212.2 %reduce-scatter.12.cloned.1.call-start = ((), (), s32[]{:S(2)}) async-start(), calls=%async_computation.11 | async-start | bytes 7798784 | tf_op jit(solution)/shard_map/reduce_scatter | solution.py:96
  213.1 1.7 copy-start.18
  220.3 113.2 %reduce-scatter.14.cloned.1.call-start = ((), (), s32[]{:S(2)}) async-start(), calls=%async_computation.12 | async-start | bytes 393216 | tf_op jit(solution)/shard_map/reduce_scatter | solution.py:204
  310.8 3.4 copy-start.5
  312.2 5.9 copy-start.30
  318.2 2.5 copy-start.15
  321.9 109.9 %reduce-scatter.18.cloned.1.call-start = ((), (), s32[]{:S(2)}) async-start(), calls=%async_computation.15 | async-start | bytes 3411968
  324.3 1.5 copy-start.23
  324.3 180.8 %reduce-scatter.16.cloned.1.call-start = ((), (), s32[]{:S(2)}) async-start(), calls=%async_computation.14 | async-start | bytes 4386816
  325.7 8.9 %copy-start.17 = (bf16[128,896]{1,0:T(8,128)(2,1)S(1)}, bf16[128,896]{1,0:T(8,128)(2,1)}, u32[]{:S(2)}) copy-start(bf16[128,896]{1,0:T(8,128)(2,1)} %copy-done.16) | copy-start | bytes 688132
  325.8 11.6 %copy-start.7 = (f32[128,2,7,64]{0,3,2,1:T(8,128)}, f32[128,2,7,64]{0,3,2,1:T(8,128)S(1)}, u32[]{:S(2)}) copy-start(f32[128,2,7,64]{0,3,2,1:T(8,128)S(1)} %maximum_add_fusion) | copy-start | bytes 1376260
  334.5 2.9 copy-start.26
  334.5 2.9 copy-start.24
  334.6 2.8 copy-start.8
  337.4 262.8 %reduce-scatter.10.cloned.1.call-start = ((), (), s32[]{:S(2)}) async-start(), calls=%async_computation.10 | async-start | bytes 7798784 | tf_op jit(solution)/shard_map/reduce_scatter | solution.py:96
  351.6 62.8 %all-to-all-start.1 = ((f32[16,56,608]{2,1,0:T(8,128)}), f32[16,56,608]{2,1,0:T(8,128)S(1)}, u32[]{:S(2)}, u32[]{:S(2)}) async-start(f32[16,56,608]{2,1,0:T(8,128)} %bitcast.133), calls=%async_computation.4 | async-start | bytes 4587520 | tf_op jit(solution)/shard_map/all_to_all | solution.py:78
  357.1 344.4 %all-reduce.14.cloned.1.call-start = ((), (), s32[]{:S(2)}) async-start(), calls=%async_computation.16 | async-start | bytes 7454720 | tf_op jit(solution)/shard_map/psum | solution.py:241
  505.1 2.8 copy-start.3
  505.1 95.1 %copy-start.13 = (bf16[1,128,896]{2,1,0:T(8,128)(2,1)S(1)}, bf16[1,128,896]{2,1,0:T(8,128)(2,1)}, u32[]{:S(2)}) copy-start(bf16[1,128,896]{2,1,0:T(8,128)(2,1)} %param.12) | copy-start | bytes 688132
  704.8 3.2 copy-start.19
  (10 other events, 11.1 us)
Sparse Core Ops, SparseCore 0:
  10.2 44.2 all-gather.5
  56.7 38.4 all-gather.7
  98.1 59.2 all-gather.9
  159.6 46.7 all-gather.11
  220.5 90.3 reduce-scatter.11
  322.0 11.5 reduce-scatter.13
  337.4 94.2 reduce-scatter.17
  435.7 69.3 reduce-scatter.15
  509.1 91.1 reduce-scatter.9
  603.2 98.3 all-reduce.13

commit v2 on v1

--- a/solution.py
+++ b/solution.py
@@ -93,7 +93,29 @@
 
 
 def scatter_tokens(partial):
-    return lax.psum_scatter(partial, "seq", scatter_dimension=0, tiled=True)
+    total = lax.psum_scatter(to_bf16(partial), "seq", scatter_dimension=0, tiled=True)
+    return total.astype(jnp.float32)
+
+
+def packed_height(depth):
+    return (depth + 16) // 16 * 16
+
+
+def other(values):
+    return lax.ppermute(values, "ctx", [(0, 1), (1, 0)])
+
+
+def sum_rounded(values):
+    if lax.axis_size("ctx") != 2:
+        return lax.psum(values, "ctx")
+    mine = to_bf16(values)
+    return mine.astype(jnp.float32) + other(mine).astype(jnp.float32)
+
+
+def sum_ctx(values):
+    if lax.axis_size("ctx") != 2:
+        return lax.psum(values, "ctx")
+    return values + other(values)
 
 
 def shards(
@@ -109,17 +131,26 @@
     ffn_gain,
 ):
     f32 = jnp.float32
-    gathered = (
-        lax.all_gather(qkv_weight, "seq", axis=0, tiled=True),
-        lax.all_gather(qkv_bias, "seq", axis=0, tiled=True),
-        lax.all_gather(out_weight, "seq", axis=0, tiled=True),
-        lax.all_gather(attn_gain, "seq", axis=0, tiled=True),
-        lax.all_gather(ffn_gain, "seq", axis=0, tiled=True),
-    )
-    full_qkv, full_bias, full_out, gain_one, gain_two = gathered
+    qkv_columns = qkv_weight.shape[1]
+    depth = qkv_weight.shape[0]
+    bias_count = qkv_bias.shape[0]
+    packed_rows = packed_height(depth)
+    pair = jnp.concatenate([qkv_weight, out_weight], 1)
+    extra = jnp.concatenate([qkv_bias, attn_gain, ffn_gain])
+    extra = jnp.pad(extra, (0, pair.shape[1] - extra.shape[0]))[None]
+    packed = jnp.concatenate(
+        [pair, extra, jnp.zeros((packed_rows - depth - 1, pair.shape[1]), pair.dtype)], 0
+    )
+    packed = lax.all_gather(packed, "seq", axis=0, tiled=True).reshape(-1, packed_rows, pair.shape[1])
+    full_qkv = packed[:, :depth, :qkv_columns].reshape(-1, qkv_columns)
+    full_out = packed[:, :depth, qkv_columns:].reshape(-1, out_weight.shape[1])
+    full_bias = packed[:, depth, :bias_count].reshape(-1)
+    gain_one = packed[:, depth, bias_count : bias_count + depth].reshape(-1)
+    gain_two = packed[:, depth, bias_count + depth : bias_count + 2 * depth].reshape(-1)
     parts = lax.axis_size("seq")
     hidden = down_weight.shape[0]
     own_gate_up = columns_from_rows(gate_up_weight, parts)
+    own_gate_up, full_qkv = lax.optimization_barrier((own_gate_up, full_qkv))
     all_cot = lax.all_gather(cotangent[0], "seq", axis=0, tiled=True)
     inputs_f = tokens[0].astype(f32)
     cot_row = cotangent[0]
@@ -148,10 +179,16 @@
     query_rot = to_bf16(query * cos_query + rotate_half(query) * sin_query)
     key_rot = to_bf16(keys * cos_key + rotate_half(keys) * sin_key).reshape(row_count, key_width)
     value_b = to_bf16(values)
-    all_keys, all_values = (
-        lax.all_gather(key_rot, "ctx", axis=0, tiled=True),
-        lax.all_gather(value_b, "ctx", axis=0, tiled=True),
-    )
+    both = jnp.concatenate([key_rot, value_b], -1)
+    if lax.axis_size("ctx") == 2:
+        both = jnp.concatenate([both, other(both)], 0)
+        other_row = lax.dynamic_slice_in_dim(
+            all_positions, (1 - lax.axis_index("ctx")) * row_count, row_count, 0
+        )
+        all_positions = jnp.concatenate([position_row, other_row])
+    else:
+        both = lax.all_gather(both, "ctx", axis=0, tiled=True)
+    all_keys, all_values = both[:, :key_width], both[:, key_width:]
     all_keys = all_keys.reshape(-1, KV_HEADS, HEAD_DIM)
     all_values = all_values.reshape(-1, KV_HEADS, HEAD_DIM)
     scores = (
@@ -184,8 +221,10 @@
     output_row = (
         residual + scatter_tokens(jnp.dot(activated, down_weight, preferred_element_type=f32))
     ).astype(jnp.bfloat16)
-    down_grad = contract_rows(activated, all_cot)
-    gate_up_grad = rows_from_columns(contract_rows(all_second, grad_gate_up), parts)
+    result_down = sum_rounded(contract_rows(activated, all_cot))
+    result_gate_up = rows_from_columns(
+        to_bf16(sum_rounded(contract_rows(all_second, grad_gate_up))), parts
+    ).astype(f32)
     grad_through, gain_two_grad = rms_backward(
         grad_second, normed_two, scale_two, gain_two.astype(f32)
     )
@@ -201,18 +240,17 @@
     grad_query_rot = jnp.einsum("kgts,skd->tkgd", grad_scores, all_keys, preferred_element_type=f32)
     key_part = jnp.einsum("kgts,tkgd->skd", grad_scores, query_rot, preferred_element_type=f32)
     value_part = jnp.einsum("kgts,tkgd->skd", probs_b, grad_attended, preferred_element_type=f32)
-    key_local = lax.psum_scatter(
-        jnp.concatenate(
-            [
-                key_part.reshape(row_count * lax.axis_size("ctx"), key_width),
-                value_part.reshape(row_count * lax.axis_size("ctx"), key_width),
-            ],
-            -1,
-        ),
-        "ctx",
-        scatter_dimension=0,
-        tiled=True,
-    )
+    key_parts = jnp.concatenate(
+        [
+            key_part.reshape(row_count * lax.axis_size("ctx"), key_width),
+            value_part.reshape(row_count * lax.axis_size("ctx"), key_width),
+        ],
+        -1,
+    )
+    if lax.axis_size("ctx") == 2:
+        key_local = key_parts[:row_count] + other(key_parts[row_count:])
+    else:
+        key_local = lax.psum_scatter(key_parts, "ctx", scatter_dimension=0, tiled=True)
     grad_key_rot = key_local[:, :key_width].reshape(row_count, KV_HEADS, HEAD_DIM)
     grad_value = key_local[:, key_width:]
     grad_query = grad_query_rot * cos_query + rotate_back(grad_query_rot * sin_query)
@@ -227,30 +265,35 @@
     )
     bias_grad = jnp.sum(grad_projected, axis=0)
     grad_proj_b = to_bf16(grad_projected)
-    qkv_grad = weight_rows(first_in, grad_proj_b)
     grad_first = jnp.dot(grad_proj_b, full_qkv.T, preferred_element_type=f32)
     grad_input_part, gain_one_grad = rms_backward(
         grad_first, normed_one, scale_one, gain_one.astype(f32)
     )
     input_row_grad = grad_residual + grad_input_part
-    bias_share, gain_one_share, gain_two_share = (
-        lax.psum_scatter(bias_grad, "seq", scatter_dimension=0, tiled=True),
-        lax.psum_scatter(gain_one_grad, "seq", scatter_dimension=0, tiled=True),
-        lax.psum_scatter(gain_two_grad, "seq", scatter_dimension=0, tiled=True),
-    )
-    summed = lax.psum(
-        (qkv_grad, bias_share, out_grad, gate_up_grad, down_grad, gain_one_share, gain_two_share),
-        "ctx",
-    )
-    (
-        result_qkv,
-        result_bias,
-        result_out,
-        result_gate_up,
-        result_down,
-        result_gain_one,
-        result_gain_two,
-    ) = summed
+    small = jnp.concatenate(
+        [
+            bias_grad.reshape(parts, -1),
+            gain_one_grad.reshape(parts, -1),
+            gain_two_grad.reshape(parts, -1),
+        ],
+        -1,
+    )
+    small = jnp.pad(small, ((0, 0), (0, qkv_columns - small.shape[1])))[:, None]
+    grad_rows = (depth + 8) // 8 * 8
+    packed_grad = jnp.concatenate(
+        [
+            contract_rows(first_in, grad_proj_b).reshape(parts, depth, qkv_columns),
+            small,
+            jnp.zeros((parts, grad_rows - depth - 1, qkv_columns), f32),
+        ],
+        1,
+    ).reshape(parts * grad_rows, qkv_columns)
+    packed_sum = sum_ctx(lax.psum_scatter(packed_grad, "seq", scatter_dimension=0, tiled=True))
+    result_qkv = packed_sum[:depth]
+    result_bias = packed_sum[depth, :bias_count]
+    result_gain_one = packed_sum[depth, bias_count : bias_count + depth]
+    result_gain_two = packed_sum[depth, bias_count + depth : bias_count + 2 * depth]
+    result_out = sum_ctx(out_grad)
     return (
         output_row[None],
         input_row_grad[None],

time: 717 us -> 541 us (0.75)
  blocking collectives: 158 us -> 0 us
  waiting for transfers between devices: 422 us -> 398 us
  starting transfers between devices: 6.19 us -> 20.6 us
    psum x1 -> x0, waiting for transfers between devices: 98.9 us -> none  [shards(): lax.psum((qkv_grad, bias_share, out_grad, gate_up_grad, down_grad, gain_o...]
    unnamed x2 -> x0, blocking collectives: 95.3 us -> none
    all_to_all x1 -> x0, blocking collectives: 48.1 us -> none  [columns_from_rows(): lax.all_to_all(split, 'seq', split_axis=0, concat_axis=0, tiled=True)]
    all_gather x1, waiting for transfers between devices: 0.01 us -> 44.7 us  [shards(): all_second = lax.all_gather(second_in, 'seq', axis=0, tiled=True)]
    all_to_all x1, waiting for transfers between devices: 52.4 us -> 11.3 us  [rows_from_columns(): lax.all_to_all(split, 'seq', split_axis=0, concat_axis=0, tiled=True)]
    ppermute x0 -> x6, waiting for transfers between devices: none -> 38.5 us  [other(): return lax.ppermute(values, 'ctx', [(0, 1), (1, 0)])]
    all_gather x2 -> x1, waiting for transfers between devices: 27.2 us -> 51.3 us  [shards(): lax.all_gather(packed, 'seq', axis=0, tiled=True)]
    reduce_scatter x3, waiting for transfers between devices: 122 us -> 141 us  [the longest x2 137 us: scatter_tokens(): lax.psum_scatter(to_bf16(partial), 'seq', scatter_dimension=0, tiled=True)]
  transfers between devices with their start and end apart: 11 -> 15, of which waited for: 10 -> 11; matrix products, arithmetic and copies ran while one was open for 10% -> 11% of each run, Pallas kernels for 0% -> 0%
where the time goes in v2:
time: 541 us; the launch traced here: 540 us
  waiting for transfers between devices  398 us (74%)
  matrix products  49.7 us (9%)
  local copies, waits for them, and re-layouts  36.8 us (7%)
  starting transfers between devices  20.6 us (4%)
  other arithmetic  19.5 us (4%)
  between operations  14.9 us (3%)
    reduce_scatter x2, waiting for transfers between devices, scatter_tokens(): lax.psum_scatter(to_bf16(partial), 'seq', scatter_dimension=0, tiled=True)  137 us
    unnamed x8, waiting for transfers between devices  69.8 us
    all_gather x1, waiting for transfers between devices, shards(): lax.all_gather(packed, 'seq', axis=0, tiled=True)  51.3 us
    all_gather x1, waiting for transfers between devices, shards(): all_second = lax.all_gather(second_in, 'seq', axis=0, tiled=True)  44.7 us
    all_gather x1, waiting for transfers between devices, shards(): all_cot = lax.all_gather(cotangent[0], 'seq', axis=0, tiled=True)  41.3 us
    ppermute x6, waiting for transfers between devices, other(): return lax.ppermute(values, 'ctx', [(0, 1), (1, 0)])  38.5 us
    dot_general x2, matrix products, contract_columns(): lax.dot_general(left_side, right_side, (((1,), (1,)), ((), ())), preferre...  13 us
    dot_general x3, matrix products, contract_rows(): lax.dot_general(left_side, right_side, (((0,), (0,)), ((), ())), preferre...  12.5 us
  transfers between devices with their start and end apart: 15, of which 11 were waited for; matrix products, arithmetic and copies ran while one was open for 11% of the time, Pallas kernels for 0%

profile of v2, /device:TPU:0, one launch (start us, length us, event | category | flops | bytes accessed | tf_op | source)
XLA Modules:
  0.0 540.1 jit_solution(10440751118810921936)
XLA Ops:
  8.1 1.8 maximum_maximum_fusion.1
  9.9 4.3 reshape.174
  14.3 2.4 copy.72
  16.7 1.8 reshape.175
  18.5 7.5 %all-to-all-start = ((bf16[16,56,608]{2,1,0:T(8,128)(2,1)}), bf16[16,56,608]{2,1,0:T(8,128)(2,1)}, u32[]{:S(2)}, u32[]{:S(2)}) async-start(bf16[16,56,608]{2,1,0:T(8,128)(2,1)} %reshape.175), calls=%async_computation | async-start | bytes 2293760 | tf_op jit(solution)/shard_map/all_to_all | solution.py:70
  26.5 51.3 %all-gather.5.cloned.1.call-done = bf16[1024,2048]{1,0:T(8,128)(2,1)} async-done(((bf16[64,2048]{1,0:T(8,128)(2,1)}), bf16[1024,2048]{1,0:T(8,128)(2,1)}) %all-gather.5.cloned.1.call-update) | async-done | bytes 4194320 | tf_op jit(solution)/shard_map/all_gather | solution.py:144
  86.3 2.8 slice.125
  92.9 2.0 multiply_reduce_fusion.1
  96.6 44.7 %all-gather.7.cloned.1.call-done = bf16[2048,896]{1,0:T(8,128)(2,1)} async-done(((bf16[128,896]{1,0:T(8,128)(2,1)}), bf16[2048,896]{1,0:T(8,128)(2,1)}) %all-gather.7.cloned.1.call-update) | async-done | bytes 3670032 | tf_op jit(solution)/shard_map/all_gather | solution.py:210
  141.4 7.4 %fusion.55 = f32[2048,608]{0,1:T(8,128)} fusion(bf16[2048,896]{1,0:T(8,128)(2,1)} %all-gather.7.cloned.1.call-done, bf16[896,608]{1,0:T(8,128)(2,1)} %bitcast.4), kind=kOutput, calls=%fused_computation.125 | convolution fusion | flops 2231369728 | bytes 9740288 | tf_op jit(solution)/shard_map/dot_general | solution.py:211
  148.7 41.3 %all-gather.9.cloned.1.call-done = bf16[1,2048,896]{2,1,0:T(8,128)(2,1)} async-done(((bf16[1,128,896]{2,1,0:T(8,128)(2,1)}), bf16[1,2048,896]{2,1,0:T(8,128)(2,1)}) %all-gather.9.cloned.1.call-update) | async-done | bytes 3670032 | tf_op jit(solution)/shard_map/all_gather | solution.py:154
  190.0 6.8 %multiply_convert_fusion.1 = (bf16[2048,304]{0,1:T(8,128)(2,1)S(1)}, bf16[2048,304]{0,1:T(8,128)(2,1)S(1)}, bf16[2048,304]{0,1:T(8,128)(2,1)}) fusion(f32[2048,608]{0,1:T(8,128)} %fusion.55, bf16[304,896]{1,0:T(8,128)(2,1)S(1)} %copy-done, bf16[1,2048,896]{2,1,0:T(8,128)(2,1)} %all-gather.9.cloned.1.call-done), kind=kOutput, calls=%fused_computation.10 | convolution fusion | flops 1125023744 | bytes 12931072 | tf_op jit(solution)/shard_map/dot_general | solution.py:90
  198.6 6.2 %convolution_convert_fusion.1 = bf16[2048,896]{1,0:T(8,128)(2,1)} fusion(bf16[2048,608]{0,1:T(8,128)(2,1)S(1)} %pad_maximum_fusion, bf16[896,608]{1,0:T(8,128)(2,1)} %bitcast.4), kind=kOutput, calls=%fused_computation.6 | convolution fusion | flops 2233204736 | bytes 7249920 | tf_op jit(solution)/shard_map/dot_general | solution.py:90
  205.4 66.8 %reduce-scatter.9.cloned.1.call-done = bf16[128,896]{1,0:T(8,128)(2,1)} async-done(((bf16[2048,896]{1,0:T(8,128)(2,1)}), bf16[128,896]{1,0:T(8,128)(2,1)}) %reduce-scatter.9.cloned.1.call-update) | async-done | bytes 229392 | tf_op jit(solution)/shard_map/reduce_scatter | solution.py:96
  283.3 3.3 collective-permute-done.1
  287.9 2.7 fusion.58
  290.9 4.8 maximum_maximum_fusion
  296.6 2.2 fusion.59
  299.1 5.6 %convolution_convert_fusion = bf16[2048,896]{1,0:T(8,128)(2,1)} fusion(bf16[2048,304]{0,1:T(8,128)(2,1)} %get-tuple-element.23, bf16[304,896]{1,0:T(8,128)(2,1)S(1)} %copy-done), kind=kOutput, calls=%fused_computation.5 | convolution fusion | flops 1117519872 | bytes 5459968 | tf_op jit(solution)/shard_map/dot_general | solution.py:222
  304.7 5.9 %convolution_convert_fusion.2 = bf16[896,608]{0,1:T(8,128)(2,1)S(1)} fusion(bf16[2048,608]{0,1:T(8,128)(2,1)} %copy-done.6, bf16[2048,896]{1,0:T(8,128)(2,1)} %all-gather.7.cloned.1.call-done), kind=kOutput, calls=%fused_computation.23 | convolution fusion | flops 2231914496 | bytes 7249920 | tf_op jit(solution)/shard_map/dot_general | solution.py:84
  312.0 21.8 %collective-permute-done.4 = bf16[896,608]{0,1:T(8,128)(2,1)S(1)} collective-permute-done((bf16[896,608]{0,1:T(8,128)(2,1)S(1)}, bf16[896,608]{0,1:T(8,128)(2,1)S(1)}, u32[]{:S(2)}, u32[]{:S(2)}) %collective-permute-start.4) | collective-permute-done | bytes 1089568 | tf_op jit(solution)/shard_map/ppermute | solution.py:105
  335.5 3.7 all-to-all-start.1
  339.3 4.0 fusion.9
  344.7 13.3 %collective-permute-done.5 = bf16[304,896]{1,0:T(8,128)(2,1)S(1)} collective-permute-done((bf16[304,896]{1,0:T(8,128)(2,1)S(1)}, bf16[304,896]{1,0:T(8,128)(2,1)S(1)}, u32[]{:S(2)}, u32[]{:S(2)}) %collective-permute-start.5) | collective-permute-done | bytes 544800 | tf_op jit(solution)/shard_map/ppermute | solution.py:105
  359.1 11.3 %all-to-all-done.1 = bf16[16,56,608]{2,1,0:T(8,128)(2,1)S(1)} async-done(((bf16[16,56,608]{2,1,0:T(8,128)(2,1)}), bf16[16,56,608]{2,1,0:T(8,128)(2,1)S(1)}, u32[]{:S(2)}, u32[]{:S(2)}) %all-to-all-start.1) | async-done | bytes 1089568 | tf_op jit(solution)/shard_map/all_to_all | solution.py:78
  370.4 3.1 reshape.201
  373.5 4.2 copy.62
  377.7 4.3 reshape.200
  382.0 4.8 reduce-scatter.11.cloned.1.call-done
  388.3 69.0 %reduce-scatter.13.cloned.1.call-done = f32[56,896]{1,0:T(8,128)} async-done(((f32[896,896]{1,0:T(8,128)}), f32[56,896]{1,0:T(8,128)}) %reduce-scatter.13.cloned.1.call-update) | async-done | bytes 200720
  458.8 69.9 %reduce-scatter.7.cloned.1.call-done = bf16[128,896]{1,0:T(8,128)(2,1)} async-done(((bf16[2048,896]{1,0:T(8,128)(2,1)}), bf16[128,896]{1,0:T(8,128)(2,1)}) %reduce-scatter.7.cloned.1.call-update) | async-done | bytes 229392 | tf_op jit(solution)/shard_map/reduce_scatter | solution.py:96
  528.6 2.0 fusion.28
  (165 shorter events, 42.1 us)
Async XLA Ops:
  7.2 182.9 %copy-start = (bf16[304,896]{1,0:T(8,128)(2,1)S(1)}, bf16[304,896]{1,0:T(8,128)(2,1)}, u32[]{:S(2)}) copy-start(bf16[304,896]{1,0:T(8,128)(2,1)} %param.17) | copy-start | bytes 1634308
  7.2 70.7 %all-gather.5.cloned.1.call-start = ((), (), s32[]{:S(2)}) async-start(), calls=%async_computation.6 | async-start | bytes 4456448 | tf_op jit(solution)/shard_map/all_gather | solution.py:144
  16.7 9.4 %copy-start.28 = (s32[1,256]{1,0:T(1,128)S(1)}, s32[1,256]{1,0:T(1,128)}, u32[]{:S(2)}) copy-start(s32[1,256]{1,0:T(1,128)} %param.11) | copy-start | bytes 3076
  16.7 9.6 %copy-start.5 = (bf16[1,128,896]{2,1,0:T(8,128)(2,1)S(1)}, bf16[1,128,896]{2,1,0:T(8,128)(2,1)}, u32[]{:S(2)}) copy-start(bf16[1,128,896]{2,1,0:T(8,128)(2,1)} %param.10) | copy-start | bytes 688132
  18.5 63.1 %all-to-all-start = ((bf16[16,56,608]{2,1,0:T(8,128)(2,1)}), bf16[16,56,608]{2,1,0:T(8,128)(2,1)}, u32[]{:S(2)}, u32[]{:S(2)}) async-start(bf16[16,56,608]{2,1,0:T(8,128)(2,1)} %reshape.175), calls=%async_computation | async-start | bytes 2293760 | tf_op jit(solution)/shard_map/all_to_all | solution.py:70
  26.0 115.4 %all-gather.7.cloned.1.call-start = ((), (), s32[]{:S(2)}) async-start(), calls=%async_computation.7 | async-start | bytes 3899392 | tf_op jit(solution)/shard_map/all_gather | solution.py:210
  26.3 59.9 %copy-start.16 = (f32[128,64]{0,1:T(8,128)}, f32[128,64]{0,1:T(8,128)S(1)}, u32[]{:S(2)}) copy-start(f32[128,64]{0,1:T(8,128)S(1)} %get-tuple-element.52) | copy-start | bytes 98308
  26.3 59.9 %copy-start.19 = (f32[128,64]{0,1:T(8,128)}, f32[128,64]{0,1:T(8,128)S(1)}, u32[]{:S(2)}) copy-start(f32[128,64]{0,1:T(8,128)S(1)} %get-tuple-element.51) | copy-start | bytes 98308
  79.6 3.4 copy-start.1
  83.4 5.8 %collective-permute-start = (bf16[128,256]{1,0:T(8,128)(2,1)S(1)}, bf16[128,256]{1,0:T(8,128)(2,1)S(1)}, u32[]{:S(2)}, u32[]{:S(2)}) collective-permute-start(bf16[128,256]{1,0:T(8,128)(2,1)S(1)} %pad_maximum_fusion.4), channel_id=1, source_target_pairs={{0,1},{1,0},{2,3},{3,2},{4,5},{5,4},{6,7},{7,6},{8,9},{9,8},{10,11... | collective-permute-start | bytes 196616 | tf_op jit(solution)/shard_map/ppermute | solution.py:105
  86.2 3.5 copy-start.7
  95.7 94.4 %all-gather.9.cloned.1.call-start = ((), (), s32[]{:S(2)}) async-start(), calls=%async_computation.11 | async-start | bytes 3899392 | tf_op jit(solution)/shard_map/all_gather | solution.py:154
  96.4 175.8 %reduce-scatter.9.cloned.1.call-start = ((), (), s32[]{:S(2)}) async-start(), calls=%async_computation.9 | async-start | bytes 3899392 | tf_op jit(solution)/shard_map/reduce_scatter | solution.py:96
  204.8 69.3 %copy-start.11 = (bf16[1,128,896]{2,1,0:T(8,128)(2,1)S(1)}, bf16[1,128,896]{2,1,0:T(8,128)(2,1)}, u32[]{:S(2)}) copy-start(bf16[1,128,896]{2,1,0:T(8,128)(2,1)} %param.12) | copy-start | bytes 688132
  204.8 182.0 %reduce-scatter.11.cloned.1.call-start = ((), (), s32[]{:S(2)}) async-start(), calls=%async_computation.10 | async-start | bytes 5013504 | tf_op jit(solution)/shard_map/reduce_scatter | solution.py:291
  272.2 3.7 copy-start.3
  280.2 3.0 copy-start.20
  281.5 5.1 copy-start.18
  281.5 5.0 collective-permute-start.1
  283.2 3.8 copy-start.2
  295.7 161.6 %reduce-scatter.13.cloned.1.call-start = ((), (), s32[]{:S(2)}) async-start(), calls=%async_computation.12 | async-start | bytes 3411968
  298.9 229.8 %reduce-scatter.7.cloned.1.call-start = ((), (), s32[]{:S(2)}) async-start(), calls=%async_computation.8 | async-start | bytes 3899392 | tf_op jit(solution)/shard_map/reduce_scatter | solution.py:96
  310.6 23.3 %collective-permute-start.4 = (bf16[896,608]{0,1:T(8,128)(2,1)S(1)}, bf16[896,608]{0,1:T(8,128)(2,1)S(1)}, u32[]{:S(2)}, u32[]{:S(2)}) collective-permute-start(bf16[896,608]{0,1:T(8,128)(2,1)S(1)} %convolution_convert_fusion.2), channel_id=1, source_target_pairs={{0,1},{1,0},{2,3},{3,2},{4,5},{5,4},{6,7},{7,6},{8,9},{9,8},{10,11... | collective-permute-start | bytes 3268616 | tf_op jit(solution)/shard_map/ppermute | solution.py:105
  335.5 34.9 %all-to-all-start.1 = ((bf16[16,56,608]{2,1,0:T(8,128)(2,1)}), bf16[16,56,608]{2,1,0:T(8,128)(2,1)S(1)}, u32[]{:S(2)}, u32[]{:S(2)}) async-start(bf16[16,56,608]{2,1,0:T(8,128)(2,1)} %bitcast.48), calls=%async_computation.4 | async-start | bytes 2293760 | tf_op jit(solution)/shard_map/all_to_all | solution.py:78
  343.3 14.7 %collective-permute-start.5 = (bf16[304,896]{1,0:T(8,128)(2,1)S(1)}, bf16[304,896]{1,0:T(8,128)(2,1)S(1)}, u32[]{:S(2)}, u32[]{:S(2)}) collective-permute-start(bf16[304,896]{1,0:T(8,128)(2,1)S(1)} %fusion.9), channel_id=1, source_target_pairs={{0,1},{1,0},{2,3},{3,2},{4,5},{5,4},{6,7},{7,6},{8,9},{9,8},{10,11... | collective-permute-start | bytes 1634312 | tf_op jit(solution)/shard_map/ppermute | solution.py:105
  377.7 150.9 %copy-start.12 = (bf16[1,128,896]{2,1,0:T(8,128)(2,1)S(1)}, bf16[1,128,896]{2,1,0:T(8,128)(2,1)}, u32[]{:S(2)}) copy-start(bf16[1,128,896]{2,1,0:T(8,128)(2,1)} %param.12) | copy-start | bytes 688132
  377.7 150.9 %copy-start.15 = (bf16[128,896]{1,0:T(8,128)(2,1)S(1)}, bf16[128,896]{1,0:T(8,128)(2,1)}, u32[]{:S(2)}) copy-start(bf16[128,896]{1,0:T(8,128)(2,1)} %reduce-scatter.9.cloned.1.call-done) | copy-start | bytes 688132
  377.7 150.9 %copy-start.27 = (f32[128]{0:T(128)S(1)}, f32[128]{0:T(128)}, u32[]{:S(2)}) copy-start(f32[128]{0:T(128)} %copy-done.26) | copy-start | bytes 1540
  386.8 144.6 %copy-start.24 = (f32[64,1152]{1,0:T(8,128)S(1)}, f32[64,1152]{1,0:T(8,128)}, u32[]{:S(2)}) copy-start(f32[64,1152]{1,0:T(8,128)} %reduce-scatter.11.cloned.1.call-done) | copy-start | bytes 884740
  386.8 144.5 %collective-permute-start.2 = (f32[64,1152]{1,0:T(8,128)}, f32[64,1152]{1,0:T(8,128)S(1)}, u32[]{:S(2)}, u32[]{:S(2)}) collective-permute-start(f32[64,1152]{1,0:T(8,128)} %reduce-scatter.11.cloned.1.call-done), channel_id=1, source_target_pairs={{0,1},{1,0},{2,3},{3,2},{4,5},{5,4},{6,7},{7,6},{8,9},{9,8},{10,11... | collective-permute-start | bytes 884744 | tf_op jit(solution)/shard_map/ppermute | solution.py:105
  457.3 73.4 %copy-start.25 = (f32[56,896]{1,0:T(8,128)S(1)}, f32[56,896]{1,0:T(8,128)}, u32[]{:S(2)}) copy-start(f32[56,896]{1,0:T(8,128)} %reduce-scatter.13.cloned.1.call-done) | copy-start | bytes 602116
  457.3 73.4 %collective-permute-start.3 = (f32[56,896]{1,0:T(8,128)}, f32[56,896]{1,0:T(8,128)S(1)}, u32[]{:S(2)}, u32[]{:S(2)}) collective-permute-start(f32[56,896]{1,0:T(8,128)} %reduce-scatter.13.cloned.1.call-done), channel_id=1, source_target_pairs={{0,1},{1,0},{2,3},{3,2},{4,5},{5,4},{6,7},{7,6},{8,9},{9,8},{10,11... | collective-permute-start | bytes 602120 | tf_op jit(solution)/shard_map/ppermute | solution.py:105
  (13 other events, 19.5 us)
Sparse Core Ops, SparseCore 0:
  10.7 67.0 all-gather.4
  95.8 45.5 all-gather.6
  143.7 46.3 all-gather.8
  204.9 67.2 reduce-scatter.8
  295.8 90.9 reduce-scatter.10
  390.5 66.7 reduce-scatter.12
  461.2 67.4 reduce-scatter.6

commit v3 on v2

--- a/solution.py
+++ b/solution.py
@@ -1,6 +1,10 @@
+import functools
+
 import jax
 import jax.numpy as jnp
 from jax import lax
+from jax.experimental import pallas as pl
+from jax.experimental.pallas import tpu as pltpu
 from jax.sharding import PartitionSpec as P
 
 HEADS = 14
@@ -95,6 +99,99 @@
 def scatter_tokens(partial):
     total = lax.psum_scatter(to_bf16(partial), "seq", scatter_dimension=0, tiled=True)
     return total.astype(jnp.float32)
+
+
+def gather_kernel(outer, own_ref, all_ref, local_sem, outer_sems, middle_sems, core_sems):
+    me = lax.axis_index("seq")
+    at_outer = me // 4
+    middle = (me // 2) % 2
+    core = me % 2
+    rows = own_ref.shape[0]
+
+    def place(outer_at, middle_at, core_at):
+        index = outer_at * 4 + middle_at * 2 + core_at
+        return all_ref.at[pl.ds(pl.multiple_of(index * rows, rows), rows)]
+
+    def remote(source, target, sems, slot, device):
+        return pltpu.make_async_remote_copy(
+            src_ref=source,
+            dst_ref=target,
+            send_sem=sems.at[0, slot],
+            recv_sem=sems.at[1, slot],
+            device_id={"seq": device},
+            device_id_type=pl.DeviceIdType.MESH,
+        )
+
+    middle_partner = at_outer * 4 + (1 - middle) * 2 + core
+    core_partner = at_outer * 4 + middle * 2 + (1 - core)
+    outer_partners = [
+        ((at_outer + step) % outer) * 4 + middle * 2 + core for step in range(1, outer)
+    ]
+    barrier = pltpu.get_barrier_semaphore()
+    for device in [middle_partner, core_partner] + outer_partners:
+        pl.semaphore_signal(
+            barrier, inc=1, device_id={"seq": device}, device_id_type=pl.DeviceIdType.MESH
+        )
+    pl.semaphore_wait(barrier, outer + 1)
+
+    own_place = place(at_outer, middle, core)
+    local = pltpu.make_async_copy(own_ref, own_place, local_sem)
+    local.start()
+    started = []
+    outer_copies = []
+    for step in range(1, outer):
+        copy = remote(own_ref, own_place, outer_sems, step - 1, outer_partners[step - 1])
+        copy.start()
+        outer_copies.append(copy)
+    middle_copies = []
+    for step in range(outer):
+        source_outer = (at_outer + outer - step) % outer
+        here = place(source_outer, middle, core)
+        if step == 0:
+            source = own_ref
+        else:
+            outer_copies[step - 1].wait_recv()
+            source = here
+        copy = remote(source, here, middle_sems, step, middle_partner)
+        copy.start()
+        middle_copies.append(copy)
+        copy = remote(source, here, core_sems, 2 * step, core_partner)
+        copy.start()
+        started.append(copy)
+    for step in range(outer):
+        source_outer = (at_outer + outer - step) % outer
+        middle_copies[step].wait_recv()
+        here = place(source_outer, 1 - middle, core)
+        copy = remote(here, here, core_sems, 2 * step + 1, core_partner)
+        copy.start()
+        started.append(copy)
+    for copy in started:
+        copy.wait_recv()
+    for copy in outer_copies + middle_copies + started:
+        copy.wait_send()
+    local.wait()
+
+
+def gather_rows(rows, collective_id):
+    parts = lax.axis_size("seq")
+    if parts % 4:
+        return lax.all_gather(rows, "seq", axis=0, tiled=True)
+    outer = parts // 4
+    return pl.pallas_call(
+        functools.partial(gather_kernel, outer),
+        out_shape=jax.ShapeDtypeStruct((parts * rows.shape[0], rows.shape[1]), rows.dtype),
+        in_specs=[pl.BlockSpec(memory_space=pltpu.VMEM)],
+        out_specs=pl.BlockSpec(memory_space=pltpu.VMEM),
+        scratch_shapes=[
+            pltpu.SemaphoreType.DMA,
+            pltpu.SemaphoreType.DMA((2, max(outer - 1, 1))),
+            pltpu.SemaphoreType.DMA((2, outer)),
+            pltpu.SemaphoreType.DMA((2, 2 * outer)),
+        ],
+        compiler_params=pltpu.CompilerParams(
+            collective_id=collective_id, has_side_effects=True, vmem_limit_bytes=24 * 2**20
+        ),
+    )(rows)
 
 
 def packed_height(depth):
@@ -150,8 +247,8 @@
     parts = lax.axis_size("seq")
     hidden = down_weight.shape[0]
     own_gate_up = columns_from_rows(gate_up_weight, parts)
-    own_gate_up, full_qkv = lax.optimization_barrier((own_gate_up, full_qkv))
-    all_cot = lax.all_gather(cotangent[0], "seq", axis=0, tiled=True)
+    all_cot = gather_rows(cotangent[0], 0)
+    own_gate_up, all_cot, full_qkv = lax.optimization_barrier((own_gate_up, all_cot, full_qkv))
     inputs_f = tokens[0].astype(f32)
     cot_row = cotangent[0]
     row_count = inputs_f.shape[0]
@@ -207,7 +304,7 @@
     residual = inputs_f + jnp.dot(attended_flat, full_out, preferred_element_type=f32)
     normed_two, scale_two = rms_forward(residual)
     second_in = to_bf16(normed_two * gain_two.astype(f32))
-    all_second = lax.all_gather(second_in, "seq", axis=0, tiled=True)
+    all_second = gather_rows(second_in, 1)
     gate_up = jnp.dot(all_second, own_gate_up, preferred_element_type=f32)
     gate = gate_up[:, :hidden]
     upward = gate_up[:, hidden:]

time: 541 us -> 516 us (0.954)
  waiting for transfers between devices: 398 us -> 265 us
  Pallas kernels: 0 us -> 113 us
  matrix products: 49.7 us -> 43.5 us
    pallas_call x0 -> x2, Pallas kernels: none -> 113 us  [gather_rows(): pl.pallas_call(functools.partial(gather_kernel, outer), out_shape=jax.Sha...]
    all_gather x2 -> x0, waiting for transfers between devices: 86 us -> none  [the longest x1 44.7 us: shards(): all_second = lax.all_gather(second_in, 'seq', axis=0, tiled=True)]
    all_gather x1, waiting for transfers between devices: 51.3 us -> 0.02 us  [shards(): lax.all_gather(packed, 'seq', axis=0, tiled=True)]
    unnamed x8 -> x6, waiting for transfers between devices: 69.8 us -> 69.2 us
  transfers between devices with their start and end apart: 15 -> 13, of which waited for: 11 -> 8; matrix products, arithmetic and copies ran while one was open for 11% -> 10% of each run, Pallas kernels for 0% -> 15%
where the time goes in v3:
time: 516 us; the launch traced here: 515 us
  waiting for transfers between devices  265 us (51%)
  Pallas kernels  113 us (22%)
  matrix products  43.5 us (8%)
  local copies, waits for them, and re-layouts  38.3 us (7%)
  starting transfers between devices  20.9 us (4%)
  other arithmetic  18.7 us (4%)
  between operations  14.8 us (3%)
    reduce_scatter x2, waiting for transfers between devices, scatter_tokens(): lax.psum_scatter(to_bf16(partial), 'seq', scatter_dimension=0, tiled=True)  142 us
    pallas_call x2, Pallas kernels, gather_rows(): pl.pallas_call(functools.partial(gather_kernel, outer), out_shape=jax.Sha...  113 us
    unnamed x6, waiting for transfers between devices  69.2 us
    ppermute x6, waiting for transfers between devices, other(): return lax.ppermute(values, 'ctx', [(0, 1), (1, 0)])  38.3 us
    dot_general x3, matrix products, contract_rows(): lax.dot_general(left_side, right_side, (((0,), (0,)), ((), ())), preferre...  12.5 us
    convert_element_type x3, local copies, waits for them, and re-layouts, shards(): result_gate_up = rows_from_columns(to_bf16(sum_rounded(contract_rows(all_...  11.6 us
    all_to_all x1, waiting for transfers between devices, rows_from_columns(): lax.all_to_all(split, 'seq', split_axis=0, concat_axis=0, tiled=True)  11.5 us
  transfers between devices with their start and end apart: 13, of which 8 were waited for; matrix products, arithmetic and copies ran while one was open for 10% of the time, Pallas kernels for 15%

profile of v3, /device:TPU:0, one launch (start us, length us, event | category | flops | bytes accessed | tf_op | source)
XLA Modules:
  0.0 515.0 jit_solution(10730015230525157402)
XLA Ops:
  8.1 1.8 maximum_maximum_fusion.1
  9.9 3.6 reshape.174
  14.7 1.9 reshape.175
  16.5 7.5 %all-to-all-start = ((bf16[16,56,608]{2,1,0:T(8,128)(2,1)}), bf16[16,56,608]{2,1,0:T(8,128)(2,1)}, u32[]{:S(2)}, u32[]{:S(2)}) async-start(bf16[16,56,608]{2,1,0:T(8,128)(2,1)} %reshape.175), calls=%async_computation | async-start | bytes 2293760 | tf_op jit(solution)/shard_map/all_to_all | solution.py:74
  24.3 79.6 %shard_map.169 = bf16[2048,896]{1,0:T(8,128)(2,1)S(1)} custom-call(bf16[128,896]{1,0:T(8,128)(2,1)S(1)} %bitcast.126), custom_call_target="tpu_custom_call" | custom-call | tf_op jit(solution)/shard_map/pallas_call | solution.py:180
  103.9 1.8 copy-done.1
  106.1 1.8 slice.114
  114.6 2.8 slice.125
  122.1 2.1 multiply_reduce_fusion.1
  124.3 33.9 %shard_map.170 = bf16[2048,896]{1,0:T(8,128)(2,1)S(1)} custom-call(bf16[128,896]{1,0:T(8,128)(2,1)S(1)} %multiply_convert_fusion.3.own_ref), custom_call_target="tpu_custom_call" | custom-call | tf_op jit(solution)/shard_map/pallas_call | solution.py:180
  158.2 5.1 fusion.48
  163.3 3.3 multiply_convert_fusion.1
  168.1 6.2 %convolution_convert_fusion.1 = bf16[2048,896]{1,0:T(8,128)(2,1)} fusion(bf16[2048,608]{0,1:T(8,128)(2,1)S(1)} %pad_maximum_fusion, bf16[896,608]{1,0:T(8,128)(2,1)} %bitcast.4), kind=kOutput, calls=%fused_computation.2 | convolution fusion | flops 2233204736 | bytes 7249920 | tf_op jit(solution)/shard_map/dot_general | solution.py:94
  175.2 71.8 %reduce-scatter.9.cloned.1.call-done = bf16[128,896]{1,0:T(8,128)(2,1)} async-done(((bf16[2048,896]{1,0:T(8,128)(2,1)}), bf16[128,896]{1,0:T(8,128)(2,1)}) %reduce-scatter.9.cloned.1.call-update) | async-done | bytes 229392 | tf_op jit(solution)/shard_map/reduce_scatter | solution.py:100
  257.7 3.4 collective-permute-done.1
  263.3 2.7 fusion.51
  266.2 4.8 maximum_maximum_fusion
  272.0 2.2 fusion.52
  274.3 5.4 %convolution_convert_fusion = bf16[2048,896]{1,0:T(8,128)(2,1)} fusion(bf16[2048,304]{0,1:T(8,128)(2,1)} %get-tuple-element.25, bf16[304,896]{1,0:T(8,128)(2,1)S(1)} %copy-done), kind=kOutput, calls=%fused_computation.1 | convolution fusion | flops 1117519872 | bytes 5459968 | tf_op jit(solution)/shard_map/dot_general | solution.py:319
  279.8 5.9 %convolution_convert_fusion.2 = bf16[896,608]{0,1:T(8,128)(2,1)S(1)} fusion(bf16[2048,608]{0,1:T(8,128)(2,1)} %copy-done.14, bf16[2048,896]{1,0:T(8,128)(2,1)} %copy-done.3), kind=kOutput, calls=%fused_computation.19 | convolution fusion | flops 2231914496 | bytes 7249920 | tf_op jit(solution)/shard_map/dot_general | solution.py:88
  287.1 21.9 %collective-permute-done.4 = bf16[896,608]{0,1:T(8,128)(2,1)S(1)} collective-permute-done((bf16[896,608]{0,1:T(8,128)(2,1)S(1)}, bf16[896,608]{0,1:T(8,128)(2,1)S(1)}, u32[]{:S(2)}, u32[]{:S(2)}) %collective-permute-start.4) | collective-permute-done | bytes 1089568 | tf_op jit(solution)/shard_map/ppermute | solution.py:202
  310.8 4.0 all-to-all-start.1
  314.7 4.0 convolution_convert_fusion.3
  320.1 13.0 %collective-permute-done.5 = bf16[304,896]{1,0:T(8,128)(2,1)S(1)} collective-permute-done((bf16[304,896]{1,0:T(8,128)(2,1)S(1)}, bf16[304,896]{1,0:T(8,128)(2,1)S(1)}, u32[]{:S(2)}, u32[]{:S(2)}) %collective-permute-start.5) | collective-permute-done | bytes 544800 | tf_op jit(solution)/shard_map/ppermute | solution.py:202
  334.3 11.5 %all-to-all-done.1 = bf16[16,56,608]{2,1,0:T(8,128)(2,1)S(1)} async-done(((bf16[16,56,608]{2,1,0:T(8,128)(2,1)}), bf16[16,56,608]{2,1,0:T(8,128)(2,1)S(1)}, u32[]{:S(2)}, u32[]{:S(2)}) %all-to-all-start.1) | async-done | bytes 1089568 | tf_op jit(solution)/shard_map/all_to_all | solution.py:82
  345.7 3.1 reshape.201
  348.8 4.2 copy.62
  353.1 4.2 reshape.200
  357.3 4.9 reduce-scatter.11.cloned.1.call-done
  363.5 69.2 %reduce-scatter.13.cloned.1.call-done = f32[56,896]{1,0:T(8,128)} async-done(((f32[896,896]{1,0:T(8,128)}), f32[56,896]{1,0:T(8,128)}) %reduce-scatter.13.cloned.1.call-update) | async-done | bytes 200720
  434.2 69.7 %reduce-scatter.7.cloned.1.call-done = bf16[128,896]{1,0:T(8,128)(2,1)} async-done(((bf16[2048,896]{1,0:T(8,128)(2,1)}), bf16[128,896]{1,0:T(8,128)(2,1)}) %reduce-scatter.7.cloned.1.call-update) | async-done | bytes 229392 | tf_op jit(solution)/shard_map/reduce_scatter | solution.py:100
  503.9 2.0 fusion.21
  (179 shorter events, 41.3 us)
Async XLA Ops:
  7.2 156.1 %copy-start = (bf16[304,896]{1,0:T(8,128)(2,1)S(1)}, bf16[304,896]{1,0:T(8,128)(2,1)}, u32[]{:S(2)}) copy-start(bf16[304,896]{1,0:T(8,128)(2,1)} %param.17) | copy-start | bytes 1634308
  7.2 98.9 %all-gather.2.cloned.1.call-start = ((), (), s32[]{:S(2)}) async-start(), calls=%async_computation.6 | async-start | bytes 4456448 | tf_op jit(solution)/shard_map/all_gather | solution.py:241
  14.7 9.6 %copy-start.4 = (bf16[1,128,896]{2,1,0:T(8,128)(2,1)S(1)}, bf16[1,128,896]{2,1,0:T(8,128)(2,1)}, u32[]{:S(2)}) copy-start(bf16[1,128,896]{2,1,0:T(8,128)(2,1)} %param.12) | copy-start | bytes 688132
  16.5 93.4 %all-to-all-start = ((bf16[16,56,608]{2,1,0:T(8,128)(2,1)}), bf16[16,56,608]{2,1,0:T(8,128)(2,1)}, u32[]{:S(2)}, u32[]{:S(2)}) async-start(bf16[16,56,608]{2,1,0:T(8,128)(2,1)} %reshape.175), calls=%async_computation | async-start | bytes 2293760 | tf_op jit(solution)/shard_map/all_to_all | solution.py:74
  24.0 81.6 %copy-start.37 = (s32[1,256]{1,0:T(1,128)S(1)}, s32[1,256]{1,0:T(1,128)}, u32[]{:S(2)}) copy-start(s32[1,256]{1,0:T(1,128)} %param.11) | copy-start | bytes 3076
  24.0 81.8 %copy-start.10 = (bf16[1,128,896]{2,1,0:T(8,128)(2,1)S(1)}, bf16[1,128,896]{2,1,0:T(8,128)(2,1)}, u32[]{:S(2)}) copy-start(bf16[1,128,896]{2,1,0:T(8,128)(2,1)} %param.10) | copy-start | bytes 688132
  24.0 223.0 %reduce-scatter.9.cloned.1.call-start = ((), (), s32[]{:S(2)}) async-start(), calls=%async_computation.8 | async-start | bytes 3899392 | tf_op jit(solution)/shard_map/reduce_scatter | solution.py:100
  105.8 8.6 %copy-start.22 = (f32[128,64]{0,1:T(8,128)}, f32[128,64]{0,1:T(8,128)S(1)}, u32[]{:S(2)}) copy-start(f32[128,64]{0,1:T(8,128)S(1)} %get-tuple-element.54) | copy-start | bytes 98308
  105.9 8.6 %copy-start.25 = (f32[128,64]{0,1:T(8,128)}, f32[128,64]{0,1:T(8,128)S(1)}, u32[]{:S(2)}) copy-start(f32[128,64]{0,1:T(8,128)S(1)} %get-tuple-element.53) | copy-start | bytes 98308
  111.6 5.8 %collective-permute-start = (bf16[128,256]{1,0:T(8,128)(2,1)S(1)}, bf16[128,256]{1,0:T(8,128)(2,1)S(1)}, u32[]{:S(2)}, u32[]{:S(2)}) collective-permute-start(bf16[128,256]{1,0:T(8,128)(2,1)S(1)} %pad_maximum_fusion.4), channel_id=1, source_target_pairs={{0,1},{1,0},{2,3},{3,2},{4,5},{5,4},{6,7},{7,6},{8,9},{9,8},{10,11... | collective-permute-start | bytes 196616 | tf_op jit(solution)/shard_map/ppermute | solution.py:202
  124.2 124.2 %copy-start.31 = (f32[128]{0:T(128)}, f32[128]{0:T(128)S(1)}, u32[]{:S(2)}) copy-start(f32[128]{0:T(128)S(1)} %add_rsqrt_fusion) | copy-start | bytes 1540
  158.2 5.1 copy-start.3
  158.2 5.1 copy-start.2
  174.3 187.9 %reduce-scatter.11.cloned.1.call-start = ((), (), s32[]{:S(2)}) async-start(), calls=%async_computation.9 | async-start | bytes 5013504 | tf_op jit(solution)/shard_map/reduce_scatter | solution.py:388
  175.2 77.4 %copy-start.13 = (bf16[128,2,7,64]{0,3,2,1:T(8,128)(2,1)S(1)}, bf16[128,2,7,64]{0,3,2,1:T(8,128)(2,1)}, u32[]{:S(2)}) copy-start(bf16[128,2,7,64]{0,3,2,1:T(8,128)(2,1)} %copy-done.12) | copy-start | bytes 688132
  255.8 6.2 %copy-start.24 = (f32[128,64]{0,1:T(8,128)S(1)}, f32[128,64]{0,1:T(8,128)}, u32[]{:S(2)}) copy-start(f32[128,64]{0,1:T(8,128)} %copy-done.22) | copy-start | bytes 98308
  255.9 5.1 collective-permute-start.1
  257.6 4.8 copy-start.6
  257.6 4.8 copy-start.11
  257.6 4.8 copy-start.34
  271.1 161.6 %reduce-scatter.13.cloned.1.call-start = ((), (), s32[]{:S(2)}) async-start(), calls=%async_computation.10 | async-start | bytes 3411968
  274.2 229.7 %reduce-scatter.7.cloned.1.call-start = ((), (), s32[]{:S(2)}) async-start(), calls=%async_computation.7 | async-start | bytes 3899392 | tf_op jit(solution)/shard_map/reduce_scatter | solution.py:100
  285.6 23.4 %collective-permute-start.4 = (bf16[896,608]{0,1:T(8,128)(2,1)S(1)}, bf16[896,608]{0,1:T(8,128)(2,1)S(1)}, u32[]{:S(2)}, u32[]{:S(2)}) collective-permute-start(bf16[896,608]{0,1:T(8,128)(2,1)S(1)} %convolution_convert_fusion.2), channel_id=1, source_target_pairs={{0,1},{1,0},{2,3},{3,2},{4,5},{5,4},{6,7},{7,6},{8,9},{9,8},{10,11... | collective-permute-start | bytes 3268616 | tf_op jit(solution)/shard_map/ppermute | solution.py:202
  310.8 35.0 %all-to-all-start.1 = ((bf16[16,56,608]{2,1,0:T(8,128)(2,1)}), bf16[16,56,608]{2,1,0:T(8,128)(2,1)S(1)}, u32[]{:S(2)}, u32[]{:S(2)}) async-start(bf16[16,56,608]{2,1,0:T(8,128)(2,1)} %bitcast.47), calls=%async_computation.4 | async-start | bytes 2293760 | tf_op jit(solution)/shard_map/all_to_all | solution.py:82
  318.8 14.4 %collective-permute-start.5 = (bf16[304,896]{1,0:T(8,128)(2,1)S(1)}, bf16[304,896]{1,0:T(8,128)(2,1)S(1)}, u32[]{:S(2)}, u32[]{:S(2)}) collective-permute-start(bf16[304,896]{1,0:T(8,128)(2,1)S(1)} %convolution_convert_fusion.3), channel_id=1, source_target_pairs={{0,1},{1,0},{2,3},{3,2},{4,5},{5,4},{6,7},{7,6},{8,9},{9,8},{10,11... | collective-permute-start | bytes 1634312 | tf_op jit(solution)/shard_map/ppermute | solution.py:202
  353.1 150.9 %copy-start.21 = (bf16[128,896]{1,0:T(8,128)(2,1)S(1)}, bf16[128,896]{1,0:T(8,128)(2,1)}, u32[]{:S(2)}) copy-start(bf16[128,896]{1,0:T(8,128)(2,1)} %reduce-scatter.9.cloned.1.call-done) | copy-start | bytes 688132
  353.1 150.9 %copy-start.32 = (f32[128]{0:T(128)S(1)}, f32[128]{0:T(128)}, u32[]{:S(2)}) copy-start(f32[128]{0:T(128)} %copy-done.31) | copy-start | bytes 1540
  353.1 150.9 %copy-start.36 = (f32[128]{0:T(128)S(1)}, f32[128]{0:T(128)}, u32[]{:S(2)}) copy-start(f32[128]{0:T(128)} %copy-done.35) | copy-start | bytes 1540
  362.2 144.5 %copy-start.29 = (f32[64,1152]{1,0:T(8,128)S(1)}, f32[64,1152]{1,0:T(8,128)}, u32[]{:S(2)}) copy-start(f32[64,1152]{1,0:T(8,128)} %reduce-scatter.11.cloned.1.call-done) | copy-start | bytes 884740
  362.2 144.5 %collective-permute-start.2 = (f32[64,1152]{1,0:T(8,128)}, f32[64,1152]{1,0:T(8,128)S(1)}, u32[]{:S(2)}, u32[]{:S(2)}) collective-permute-start(f32[64,1152]{1,0:T(8,128)} %reduce-scatter.11.cloned.1.call-done), channel_id=1, source_target_pairs={{0,1},{1,0},{2,3},{3,2},{4,5},{5,4},{6,7},{7,6},{8,9},{9,8},{10,11... | collective-permute-start | bytes 884744 | tf_op jit(solution)/shard_map/ppermute | solution.py:202
  432.7 73.3 %copy-start.30 = (f32[56,896]{1,0:T(8,128)S(1)}, f32[56,896]{1,0:T(8,128)}, u32[]{:S(2)}) copy-start(f32[56,896]{1,0:T(8,128)} %reduce-scatter.13.cloned.1.call-done) | copy-start | bytes 602116
  432.7 73.3 %collective-permute-start.3 = (f32[56,896]{1,0:T(8,128)}, f32[56,896]{1,0:T(8,128)S(1)}, u32[]{:S(2)}, u32[]{:S(2)}) collective-permute-start(f32[56,896]{1,0:T(8,128)} %reduce-scatter.13.cloned.1.call-done), channel_id=1, source_target_pairs={{0,1},{1,0},{2,3},{3,2},{4,5},{5,4},{6,7},{7,6},{8,9},{9,8},{10,11... | collective-permute-start | bytes 602120 | tf_op jit(solution)/shard_map/ppermute | solution.py:202
  (20 other events, 44.1 us)
Sparse Core Ops, SparseCore 0:
  10.7 77.5 all-gather.1
  174.5 72.5 reduce-scatter.8
  271.2 90.9 reduce-scatter.10
  365.9 66.6 reduce-scatter.12
  436.4 67.5 reduce-scatter.6
